TPU v7x, 32 devices: a whole 2x2x4 slice. The times are simulated.
32 devices in a mesh: clip: 4 (over z), band: 4 (over x, core), chan: 2 (over y).
Axes of the slice: x: 2, y: 2, z: 4, core: 2. Of those that a mesh axis runs over, the one named last changes fastest.
Arguments:
- frames: bfloat16 [512, 4, 5120], P(None, 'clip', ('band', 'chan')), may hold values from -6 to 6
- weight: bfloat16 [512, 3, 3, 512], P('chan'), may hold values from -0.09375 to 0.09375
- bias: float32 [512], replicated, may hold values from -3 to 3
- cotangent: bfloat16 [512, 4, 5120], P(None, 'clip', ('band', 'chan')), may hold values from -6 to 6
Outputs:
- outputs: bfloat16 [512, 4, 5120], P(None, 'clip', ('band', 'chan'))
- grad_frames: bfloat16 [512, 4, 5120], P(None, 'clip', ('band', 'chan'))
- grad_weight: float32 [512, 3, 3, 512], P('chan')
- grad_bias: float32 [512], P('chan')
All inputs are finite; a program needn't handle non-finite values.
Results may differ from a plain program's by a relative error of at most 0.001.
Values may be sent and summed in bfloat16 or wider, within the bound.
A program may use at most 128 MiB of HBM per device.

v0:
```python
import math

import jax
import jax.numpy as jnp
from jax import lax
from jax.sharding import PartitionSpec as P

W = 160


def padded(x, sides, width):
    for axis, dim in sides:
        peers, length = (lax.axis_size(axis), x.shape[dim])
        up = [(i, (i + 1) % peers) for i in range(peers - 1)]
        down = [(j, i) for i, j in up]
        last = lax.slice_in_dim(x, length - width, length, axis=dim)
        leading = lax.slice_in_dim(x, 0, width, axis=dim)
        before = lax.ppermute(last, axis, up)
        after = lax.ppermute(leading, axis, down)
        x = jnp.concatenate([before, x, after], axis=dim)
    return x


def shifted(source, start_at, cell_count, keep_mask):
    window = lax.slice_in_dim(source, start_at, start_at + cell_count, axis=2)
    return jnp.where(keep_mask[None, None, :], window, jnp.zeros_like(window))


def local(frames, weight, bias, cotangent):
    channels, frame_count, cell_count = frames.shape
    joined = lax.axis_size("band") * lax.axis_size("chan")
    scale = 1.0 / math.sqrt(frame_count * lax.axis_size("clip") * cell_count * joined)
    first_cell = lax.axis_index(("band", "chan")) * cell_count
    column = (first_cell + jnp.arange(cell_count, dtype=jnp.int32)) % W
    left_ok = column != 0
    right_ok = column != W - 1
    every_cell = column >= 0
    keep_masks = (left_ok, every_cell, right_ok)
    margin_cells = W + 1
    stacked = jnp.stack((frames, cotangent), axis=0)
    extended = padded(stacked, ((("band", "chan"), 3),), margin_cells)
    ext_input = extended[0]
    ext_upstream = extended[1]
    in_windows = []
    cot_windows = []
    for a in range(3):
        for b in range(3):
            offset = margin_cells + (a - 1) * W + (b - 1)
            in_windows.append(shifted(ext_input, offset, cell_count, keep_masks[b]))
            back_offset = margin_cells + (1 - a) * W + (1 - b)
            cot_windows.append(shifted(ext_upstream, back_offset, cell_count, keep_masks[2 - b]))
    tap_rows = []
    for a in range(3):
        tap_row = []
        for b in range(3):
            tap_row.append(
                jnp.einsum(
                    "ifs,ofs->oi",
                    in_windows[3 * a + b],
                    cotangent,
                    preferred_element_type=jnp.float32,
                )
            )
        tap_rows.append(jnp.stack(tap_row, axis=1))
    dw_local = jnp.stack(tap_rows, axis=1) * scale
    db_local = jnp.sum(cotangent.astype(jnp.float32), axis=(1, 2)) * scale
    start_out = jnp.zeros((channels, frame_count, cell_count), jnp.float32)
    start_grad = jnp.zeros((channels, frame_count, cell_count), jnp.float32)
    kernel = lax.all_gather(weight, "chan", axis=0, tiled=True)
    conv_sum = start_out
    grad_sum = start_grad
    for a in range(3):
        for b in range(3):
            conv_sum = conv_sum + jnp.einsum(
                "ifs,oi->ofs",
                in_windows[3 * a + b],
                kernel[:, a, b, :],
                preferred_element_type=jnp.float32,
            )
            grad_sum = grad_sum + jnp.einsum(
                "ofs,oi->ifs",
                cot_windows[3 * a + b],
                kernel[:, a, b, :],
                preferred_element_type=jnp.float32,
            )
    outputs = (conv_sum + bias[:, None, None]).astype(jnp.bfloat16)
    grad_frames = grad_sum.astype(jnp.bfloat16)
    chan_count = lax.axis_size("chan")
    band_count = lax.axis_size("band")
    share_rows = channels // (chan_count * band_count)
    dw_order = dw_local.reshape(chan_count, band_count, share_rows, 3, 3, channels)
    dw_order = jnp.transpose(dw_order, (1, 0, 2, 3, 4, 5)).reshape(channels, 3, 3, channels)
    db_order = jnp.transpose(
        db_local.reshape(chan_count, band_count, share_rows), (1, 0, 2)
    ).reshape(channels)
    dw_share, db_share = (
        lax.psum_scatter(dw_order, ("band", "chan"), scatter_dimension=0, tiled=True),
        lax.psum_scatter(db_order, ("band", "chan"), scatter_dimension=0, tiled=True),
    )
    dw_share, db_share = lax.psum((dw_share, db_share), "clip")
    grad_weight, grad_bias = (
        lax.all_gather(dw_share, "band", axis=0, tiled=True),
        lax.all_gather(db_share, "band", axis=0, tiled=True),
    )
    return (outputs, grad_frames, grad_weight, grad_bias)


def solution(mesh):
    in_specs = (
        P(None, "clip", ("band", "chan")),
        P("chan", None, None, None),
        P(),
        P(None, "clip", ("band", "chan")),
    )
    out_specs = (
        P(None, "clip", ("band", "chan")),
        P(None, "clip", ("band", "chan")),
        P("chan", None, None, None),
        P("chan"),
    )
    return jax.shard_map(local, mesh=mesh, in_specs=in_specs, out_specs=out_specs, check_vma=False)
```

profile of v0, /device:TPU:0, one launch (start us, length us, event | category | flops | bytes accessed | tf_op | source)
XLA Modules:
  0.0 257.6 jit_solution(12711524196886736987)
XLA Ops:
  8.1 2.3 pad_maximum_fusion.2
  10.4 1.3 collective-permute-start.1
  11.7 5.6 %collective-permute-start = (bf16[2,512,1,161]{3,1,2,0:T(8,128)(2,1)S(1)}, bf16[2,512,1,161]{3,1,2,0:T(8,128)(2,1)S(1)}, u32[]{:S(2)}, u32[]{:S(2)}) collective-permute-start(bf16[2,512,1,161]{3,1,2,0:T(8,128)(2,1)S(1)} %get-tuple-element.22), channel_id=1, source_target_pairs={{0,1},{1,2},{2,3},{3,4},{4,5},{5,6},{6,7},{8,9},{9,10},{10,11},{11... | collective-permute-start | bytes 989192 | tf_op jit(solution)/shard_map/ppermute | solution.py:18
  17.3 10.1 %collective-permute-done.1 = bf16[2,512,1,161]{3,1,2,0:T(8,128)(2,1)S(1)} collective-permute-done((bf16[2,512,1,161]{3,1,2,0:T(8,128)(2,1)}, bf16[2,512,1,161]{3,1,2,0:T(8,128)(2,1)S(1)}, u32[]{:S(2)}, u32[]{:S(2)}) %collective-permute-start.1) | collective-permute-done | bytes 329760 | tf_op jit(solution)/shard_map/ppermute | solution.py:19
  27.4 6.4 %collective-permute-done = bf16[2,512,1,161]{3,1,2,0:T(8,128)(2,1)S(1)} collective-permute-done((bf16[2,512,1,161]{3,1,2,0:T(8,128)(2,1)S(1)}, bf16[2,512,1,161]{3,1,2,0:T(8,128)(2,1)S(1)}, u32[]{:S(2)}, u32[]{:S(2)}) %collective-permute-start) | collective-permute-done | bytes 329760 | tf_op jit(solution)/shard_map/ppermute | solution.py:18
  33.8 1.0 pad_maximum_fusion
  41.7 1.2 fusion
  42.9 4.7 %copy.18 = f32[4,2,64,3,3,512]{5,2,1,0,4,3:T(8,128)} copy(f32[4,2,64,3,3,512]{5,2,0,1,4,3:T(8,128)S(1)} %fusion) | data formatting | bytes 18874368 | tf_op jit(solution)/shard_map/transpose | solution.py:92
  47.7 82.1 %reduce-scatter.2.cloned.1.call-done = f32[64,3,3,512]{3,0,2,1:T(8,128)} async-done(((f32[512,3,3,512]{3,0,2,1:T(8,128)}), f32[64,3,3,512]{3,0,2,1:T(8,128)}) %reduce-scatter.2.cloned.1.call-update) | async-done | bytes 1179664 | tf_op jit(solution)/shard_map/reduce_scatter | solution.py:97
  130.5 57.7 %all-reduce.4.cloned.1.call-done = f32[64,3,3,512]{3,0,2,1:T(8,128)} async-done(((f32[64,3,3,512]{3,0,2,1:T(8,128)}), f32[64,3,3,512]{3,0,2,1:T(8,128)}) %all-reduce.4.cloned.1.call-update) | async-done | bytes 1179664 | tf_op jit(solution)/shard_map/psum | solution.py:100
  189.8 13.8 %all-reduce.1 = f32[512]{0:T(512)S(1)} all-reduce(f32[512]{0:T(512)S(1)} %reshape.200), channel_id=3, replica_groups=mesh['clip'=4,'band'=4,'chan'=2] {'band','chan'}, use_global_device_ids=true, to_apply=%region_3.4.clone | all-reduce | flops 512 | bytes 4096
  204.9 10.2 %psum.15 = f32[64]{0:T(128)S(1)} all-reduce(f32[64]{0:T(128)S(1)} %dynamic-slice.2), channel_id=1, replica_groups=mesh['clip'=4,'band'=4,'chan'=2] {'clip'}, use_global_device_ids=true, to_apply=%region_4.5 | all-reduce | flops 64 | bytes 512 | tf_op jit(solution)/shard_map/psum | solution.py:100
  215.4 7.0 %all-reduce = f32[256]{0:T(256)} all-reduce(f32[256]{0:T(256)S(1)} %dynamic-update-slice), channel_id=1, replica_groups=mesh['clip'=4,'band'=4,'chan'=2] {'band'}, use_global_device_ids=true, to_apply=%add | all-reduce | flops 256 | bytes 2048
  222.4 1.7 fusion.62
  224.1 1.9 convolution_add_fusion.15
  228.7 0.9 convolution_add_fusion.11
  229.6 0.9 convolution_add_fusion.10
  231.5 0.9 fusion.5
  232.4 1.1 copy.20
  233.4 2.0 fusion.23
  235.5 1.9 convolution_add_fusion.7
  237.4 1.9 convolution_add_fusion.6
  244.1 1.1 copy.21
  245.2 5.0 %copy.25 = f32[256,3,3,512]{3,0,2,1:T(8,128)} copy(f32[256,3,3,512]{3,0,2,1:T(8,128)} %all-gather.5.cloned.1.call-done) | data formatting | bytes 9437184
  (59 shorter events, 17.7 us)
Async XLA Ops:
  8.0 25.8 %copy-start.1 = (bf16[512,1,640]{2,0,1:T(8,128)(2,1)S(1)}, bf16[512,1,640]{2,0,1:T(8,128)(2,1)}, u32[]{:S(2)}) copy-start(bf16[512,1,640]{2,0,1:T(8,128)(2,1)} %param.7) | copy-start | bytes 1966084
  8.0 25.8 %copy-start.2 = (bf16[512,1,640]{2,0,1:T(8,128)(2,1)S(1)}, bf16[512,1,640]{2,0,1:T(8,128)(2,1)}, u32[]{:S(2)}) copy-start(bf16[512,1,640]{2,0,1:T(8,128)(2,1)} %param.4) | copy-start | bytes 1966084
  8.0 121.8 %reduce-scatter.2.cloned.1.call-start = ((), (), s32[]{:S(2)}) async-start(), calls=%async_computation.2 | async-start | bytes 10616832 | tf_op jit(solution)/shard_map/reduce_scatter | solution.py:97
  10.4 17.0 %collective-permute-start.1 = (bf16[2,512,1,161]{3,1,2,0:T(8,128)(2,1)}, bf16[2,512,1,161]{3,1,2,0:T(8,128)(2,1)S(1)}, u32[]{:S(2)}, u32[]{:S(2)}) collective-permute-start(bf16[2,512,1,161]{3,1,2,0:T(8,128)(2,1)} %get-tuple-element.23), channel_id=1, source_target_pairs={{1,0},{2,1},{3,2},{4,3},{5,4},{6,5},{7,6},{9,8},{10,9},{11,10},{12... | collective-permute-start | bytes 989192 | tf_op jit(solution)/shard_map/ppermute | solution.py:19
  11.7 22.2 %collective-permute-start = (bf16[2,512,1,161]{3,1,2,0:T(8,128)(2,1)S(1)}, bf16[2,512,1,161]{3,1,2,0:T(8,128)(2,1)S(1)}, u32[]{:S(2)}, u32[]{:S(2)}) collective-permute-start(bf16[2,512,1,161]{3,1,2,0:T(8,128)(2,1)S(1)} %get-tuple-element.22), channel_id=1, source_target_pairs={{0,1},{1,2},{2,3},{3,4},{4,5},{5,6},{6,7},{8,9},{9,10},{10,11},{11... | collective-permute-start | bytes 989192 | tf_op jit(solution)/shard_map/ppermute | solution.py:18
  47.7 140.5 %all-reduce.4.cloned.1.call-start = ((), (), s32[]{:S(2)}) async-start(), calls=%async_computation.3 | async-start | bytes 2359296 | tf_op jit(solution)/shard_map/psum | solution.py:100
  129.8 58.8 %copy-start.5 = (u32[32]{0:T(128)S(1)}, u32[32]{0:T(128)}, u32[]{:S(2)}) copy-start(u32[32]{0:T(128)} %constant.44) | copy-start | bytes 388
  129.8 73.8 %copy-start.4 = (u32[32]{0:T(128)S(1)}, u32[32]{0:T(128)}, u32[]{:S(2)}) copy-start(u32[32]{0:T(128)} %constant.38) | copy-start | bytes 388
  129.8 92.5 %all-gather.3.cloned.1.call-start = ((), (), s32[]{:S(2)}) async-start(), calls=%async_computation.1 | async-start | bytes 7077888 | tf_op jit(solution)/shard_map/all_gather | solution.py:69
  130.4 114.8 %all-gather.5.cloned.1.call-start = ((), (), s32[]{:S(2)}) async-start(), calls=%async_computation.4 | async-start | bytes 5898240 | tf_op jit(solution)/shard_map/all_gather | solution.py:102
  222.4 3.7 %copy-start = (bf16[512,3,3,512]{3,0,2,1:T(8,128)(2,1)S(1)}, bf16[512,3,3,512]{3,0,2,1:T(8,128)(2,1)}, u32[]{:S(2)}) copy-start(bf16[512,3,3,512]{3,0,2,1:T(8,128)(2,1)} %all-gather.3.cloned.1.call-done) | copy-start | bytes 14155780
  230.5 0.9 copy-start.3
  233.4 5.9 %slice-start = ((s8[4718592]{0:T(1024)(128)(4,1)}), s8[4194304]{0:T(1024)(128)(4,1)S(1)}, s32[]{:S(2)}) async-start(s8[4718592]{0:T(1024)(128)(4,1)} %bitcast.166), calls=%async_computation.5 | async-start | bytes 8388608
  235.5 3.9 %slice-start.1 = ((s8[4718592]{0:T(1024)(128)(4,1)}), s8[524288]{0:T(1024)(128)(4,1)S(1)}, s32[]{:S(2)}) async-start(s8[4718592]{0:T(1024)(128)(4,1)} %bitcast.166), calls=%async_computation.6 | async-start | bytes 1048576
Sparse Core Ops, SparseCore 0:
  47.8 81.9 reduce-scatter.1
  132.2 55.9 all-reduce.3
Sparse Core Ops, SparseCore 1:
  131.9 62.5 all-gather.2
  195.8 37.6 all-gather.4
where the time goes:
time: 258 us
  waiting for transfers between devices  157 us (61%)
  blocking collectives  31 us (12%)
  matrix products  27.1 us (11%)
  between operations  17.1 us (7%)
  local copies, waits for them, and re-layouts  13.8 us (5%)
  starting transfers between devices  7 us (3%)
  other arithmetic  4.74 us (2%)
    reduce_scatter x1, waiting for transfers between devices, local(): lax.psum_scatter(dw_order, ('band', 'chan'), scatter_dimension=0, tiled=T...  82.1 us
    psum x1, waiting for transfers between devices, local(): dw_share, db_share = lax.psum((dw_share, db_share), 'clip')  57.7 us
    unnamed x2, blocking collectives  20.8 us
    dot_general x9, matrix products, local(): jnp.einsum('ofs,oi->ifs', cot_windows[3 * a + b], kernel[:, a, b, :], pre...  10.6 us
    psum x1, blocking collectives, local(): dw_share, db_share = lax.psum((dw_share, db_share), 'clip')  10.2 us
    ppermute x1, waiting for transfers between devices, padded(): after = lax.ppermute(leading, axis, down)  10.1 us
    dot_general x9, matrix products, local(): jnp.einsum('ifs,oi->ofs', in_windows[3 * a + b], kernel[:, a, b, :], pref...  9.92 us
    unnamed x24, local copies, waits for them, and re-layouts  8.7 us
  transfers between devices with their start and end apart: 6, of which 4 were waited for; matrix products, arithmetic and copies ran while one was open for 10% of the time, Pallas kernels for 0%

commit v1 on v0

v1 whole, which is shorter than its diff:
```python
import functools
import math

import jax
import jax.numpy as jnp
from jax import lax
from jax.experimental import pallas as pl
from jax.experimental.pallas import tpu as pltpu
from jax.sharding import PartitionSpec as P

W = 160
MESH = pl.DeviceIdType.MESH


def ds(start, size):
    return pl.ds(pl.multiple_of(start, size), size)


def remote(src, dst, send, recv, device):
    return pltpu.make_async_remote_copy(
        src_ref=src, dst_ref=dst, send_sem=send, recv_sem=recv, device_id=device, device_id_type=MESH
    )


def position():
    return lax.axis_index("clip"), lax.axis_index("band"), lax.axis_index("chan")


def gather_kernel(dims, x_ref, g_ref, xs_ref, gs_ref, xsend, xrecv, gsend, grecv, fsend, frecv, own):
    bands, chans, rows_i, rows_o, cells = dims
    group = bands * chans
    _, b, n = position()
    me = b * chans + n
    sib = b + 1 - 2 * (b % 2)
    barrier = pltpu.get_barrier_semaphore()
    for k in range(1, group):
        to = (me + k) % group
        pl.semaphore_signal(barrier, inc=1, device_id={"band": to // chans, "chan": to % chans}, device_id_type=MESH)
    pl.semaphore_wait(barrier, group - 1)

    keep_x = pltpu.make_async_copy(x_ref.at[ds(b * rows_i, rows_i), :], xs_ref.at[:, ds(me * cells, cells)], own.at[0])
    keep_g = pltpu.make_async_copy(g_ref.at[ds(n * rows_o, rows_o), :], gs_ref.at[:, ds(me * cells, cells)], own.at[1])
    keep_x.start()
    keep_g.start()
    pairs = [(j, m) for j in range(bands // 2) for m in range(chans)]
    started = []
    for t, (j, m) in enumerate(pairs):
        if t == 0:
            continue
        to_b, to_n = (b + 2 * j) % bands, (n + m) % chans
        copy = remote(
            g_ref.at[ds(to_n * rows_o, rows_o), :], gs_ref.at[:, ds(me * cells, cells)],
            gsend.at[t], grecv.at[t], {"band": to_b, "chan": to_n},
        )
        copy.start()
        started.append(copy)
    for k in range(1, group):
        to = (me + k) % group
        to_b, to_n = to // chans, to % chans
        copy = remote(
            x_ref.at[ds(to_b * rows_i, rows_i), :], xs_ref.at[:, ds(me * cells, cells)],
            xsend.at[k], xrecv.at[k], {"band": to_b, "chan": to_n},
        )
        copy.start()
        started.append(copy)
    for t, (j, m) in enumerate(pairs):
        src = ((b + bands - 2 * j) % bands) * chans + (n + chans - m) % chans
        place = gs_ref.at[:, ds(src * cells, cells)]
        if t == 0:
            out = g_ref.at[ds(n * rows_o, rows_o), :]
        else:
            remote(place, place, gsend.at[t], grecv.at[t], {"band": sib}).wait_recv()
            out = place
        copy = remote(out, place, fsend.at[t], frecv.at[t], {"band": sib})
        copy.start()
        started.append(copy)
    for k in range(1, group):
        src = (me + group - k) % group
        place = xs_ref.at[:, ds(src * cells, cells)]
        remote(place, place, xsend.at[k], xrecv.at[k], {"band": sib}).wait_recv()
    for t, (j, m) in enumerate(pairs):
        src = ((sib + bands - 2 * j) % bands) * chans + (n + chans - m) % chans
        place = gs_ref.at[:, ds(src * cells, cells)]
        remote(place, place, fsend.at[t], frecv.at[t], {"band": sib}).wait_recv()
    for copy in started:
        copy.wait_send()
    keep_x.wait()
    keep_g.wait()


def share_kernel(
    dims, s_ref, d_ref, w_ref, lead_ref, last_ref, o_ref, db_ref, kern_ref, before_ref, after_ref,
    got, dgot, rsend, rrecv, dsend, drecv, wsend, wrecv, wfsend, wfrecv, hsend, hrecv,
    zsend, zrecv, xsend, xrecv, csend, crecv, own,
):
    clips, bands, chans, rows_o, rows_i = dims
    group = bands * chans
    taps = s_ref.shape[0]
    piece = rows_o // clips
    half = rows_o // 2
    z, b, n = position()
    me = b * chans + n
    core = b % 2
    sib = b + 1 - 2 * core
    nxt, prv = (me + 1) % group, (me + group - 1) % group
    nxt_id = {"band": nxt // chans, "chan": nxt % chans}
    prv_id = {"band": prv // chans, "chan": prv % chans}

    barrier = pltpu.get_barrier_semaphore()
    targets = [{"clip": (z + k) % clips} for k in range(1, clips)]
    targets += [{"chan": (n + m) % chans} for m in range(1, chans)]
    targets += [{"band": (b + 2 * j) % bands} for j in range(1, bands // 2)]
    targets += [{"band": sib}, nxt_id, prv_id]
    for target in targets:
        pl.semaphore_signal(barrier, inc=1, device_id=target, device_id_type=MESH)
    pl.semaphore_wait(barrier, len(targets))

    started = []

    def send(*args):
        copy = remote(*args)
        copy.start()
        started.append(copy)

    for k in range(1, clips):
        to = (z + k) % clips
        send(s_ref.at[:, ds(to * piece, piece), :], got.at[k], rsend.at[k], rrecv.at[k], {"clip": to})
        send(d_ref, dgot.at[k], dsend.at[k], drecv.at[k], {"clip": to})
    for m in range(1, chans):
        send(
            w_ref.at[:, ds(core * half, half), :], kern_ref.at[:, ds((2 * n + core) * half, half), :],
            wsend.at[m], wrecv.at[m], {"chan": (n + m) % chans},
        )
    send(last_ref, before_ref, hsend.at[0], hrecv.at[0], nxt_id)
    send(lead_ref, after_ref, hsend.at[1], hrecv.at[1], prv_id)
    keep_w = pltpu.make_async_copy(w_ref, kern_ref.at[:, ds(n * rows_o, rows_o), :], own)
    keep_w.start()

    for k in range(1, clips):
        remote(got.at[k], got.at[k], rsend.at[k], rrecv.at[k], {"band": sib}).wait_recv()
        remote(d_ref, dgot.at[k], dsend.at[k], drecv.at[k], {"band": sib}).wait_recv()

    def spot(zz, bb):
        return o_ref.at[:, ds(zz * piece, piece), ds(bb * rows_i, rows_i)]

    @pl.loop(0, taps)
    def _(t):
        total = s_ref[t, ds(z * piece, piece), :]
        for k in range(1, clips):
            total = total + got[k, t]
        o_ref[t, ds(z * piece, piece), ds(b * rows_i, rows_i)] = total

    db_total = d_ref[...]
    for k in range(1, clips):
        db_total = db_total + dgot[k]
    db_ref[...] = db_total

    width = bands // 2
    for k in range(clips):
        zz = (z + clips - k) % clips
        if k == 0:
            for q in range(1, clips):
                send(spot(z, b), spot(z, b), zsend.at[q], zrecv.at[q], {"clip": (z + q) % clips})
        else:
            remote(spot(zz, b), spot(zz, b), zsend.at[k], zrecv.at[k], {"band": sib}).wait_recv()
        for j in range(1, width):
            send(spot(zz, b), spot(zz, b), xsend.at[j, k], xrecv.at[j, k], {"band": (b + 2 * j) % bands})
        send(spot(zz, b), spot(zz, b), csend.at[0, k], crecv.at[0, k], {"band": sib})
    for m in range(1, chans):
        src = (n + chans - m) % chans
        place = kern_ref.at[:, ds((2 * src + core) * half, half), :]
        remote(place, place, wsend.at[m], wrecv.at[m], {"band": sib}).wait_recv()
        send(place, place, wfsend.at[m], wfrecv.at[m], {"band": sib})
    for k in range(clips):
        zz = (z + clips - k) % clips
        for j in range(1, width):
            bb = (b + bands - 2 * j) % bands
            remote(spot(zz, bb), spot(zz, bb), xsend.at[j, k], xrecv.at[j, k], {"band": sib}).wait_recv()
            send(spot(zz, bb), spot(zz, bb), csend.at[j, k], crecv.at[j, k], {"band": sib})
    for k in range(clips):
        zz = (z + clips - k) % clips
        for j in range(width):
            bb = (sib + bands - 2 * j) % bands
            remote(spot(zz, bb), spot(zz, bb), csend.at[j, k], crecv.at[j, k], {"band": sib}).wait_recv()
    for m in range(1, chans):
        src = (n + chans - m) % chans
        place = kern_ref.at[:, ds((2 * src + 1 - core) * half, half), :]
        remote(place, place, wfsend.at[m], wfrecv.at[m], {"band": sib}).wait_recv()
    remote(last_ref, before_ref, hsend.at[0], hrecv.at[0], {"band": sib}).wait_recv()
    remote(lead_ref, after_ref, hsend.at[1], hrecv.at[1], {"band": sib}).wait_recv()
    for copy in started:
        copy.wait_send()
    keep_w.wait()


VM = pl.BlockSpec(memory_space=pltpu.VMEM)
DMA = pltpu.SemaphoreType.DMA


def local(frames, weight, bias, cotangent):
    channels, frame_count, cells = frames.shape
    clips, bands, chans = (lax.axis_size(a) for a in ("clip", "band", "chan"))
    group = bands * chans
    assert frame_count == 1 and cells % W == 0
    total = cells * group
    scale = 1.0 / math.sqrt(frame_count * clips * total)
    rows_i, rows_o = channels // bands, channels // chans
    x = frames.reshape(channels, cells)
    g = cotangent.reshape(channels, cells)
    bf = jnp.bfloat16
    pairs = bands // 2 * chans
    xs, gs = pl.pallas_call(
        functools.partial(gather_kernel, (bands, chans, rows_i, rows_o, cells)),
        out_shape=(jax.ShapeDtypeStruct((rows_i, total), bf), jax.ShapeDtypeStruct((rows_o, total), bf)),
        in_specs=[VM, VM],
        out_specs=(VM, VM),
        scratch_shapes=[DMA((group,)), DMA((group,)), DMA((pairs,)), DMA((pairs,)), DMA((pairs,)), DMA((pairs,)), DMA((2,))],
        compiler_params=pltpu.CompilerParams(collective_id=0, has_side_effects=True),
    )(x, g)

    column = jnp.arange(total, dtype=jnp.int32) % W
    margin = jnp.zeros((rows_i, W), bf)
    zero = jnp.zeros((), bf)
    sides = []
    for b in range(3):
        moved = xs if b == 1 else jnp.roll(xs, 1 - b, axis=1)
        if b != 1:
            moved = jnp.where((column != (0 if b == 0 else W - 1))[None, :], moved, zero)
        sides.append(jnp.concatenate([margin, moved, margin], axis=1))
    sides = jnp.concatenate(sides, axis=0)
    share = []
    for a in range(3):
        window = lax.slice_in_dim(sides, a * W, a * W + total, axis=1)
        part = lax.dot_general(gs, window, (((1,), (1,)), ((), ())), preferred_element_type=jnp.float32)
        share += [part[:, b * rows_i:(b + 1) * rows_i] * scale for b in range(3)]
    share = jnp.stack(share, axis=0)
    db = jnp.sum(gs.astype(jnp.float32), axis=1) * scale
    db = jnp.broadcast_to(db[None, :], (8, rows_o))

    lead = jnp.concatenate([x[:, :W], g[:, :W]], axis=1)
    last = jnp.concatenate([x[:, cells - W:], g[:, cells - W:]], axis=1)
    wt = jnp.transpose(weight, (1, 2, 0, 3)).reshape(9, rows_o, channels)
    piece = rows_o // clips
    width = bands // 2
    grad, db, kern, before, after = pl.pallas_call(
        functools.partial(share_kernel, (clips, bands, chans, rows_o, rows_i)),
        out_shape=(
            jax.ShapeDtypeStruct((9, rows_o, channels), jnp.float32),
            jax.ShapeDtypeStruct((8, rows_o), jnp.float32),
            jax.ShapeDtypeStruct((9, channels, channels), bf),
            jax.ShapeDtypeStruct((channels, 2 * W), bf),
            jax.ShapeDtypeStruct((channels, 2 * W), bf),
        ),
        in_specs=[VM] * 5,
        out_specs=(VM,) * 5,
        scratch_shapes=[
            pltpu.VMEM((clips, 9, piece, rows_i), jnp.float32),
            pltpu.VMEM((clips, 8, rows_o), jnp.float32),
        ] + [DMA((clips,))] * 4 + [DMA((chans,))] * 4 + [DMA((2,))] * 2 + [DMA((clips,))] * 2
        + [DMA((width, clips))] * 4 + [DMA],
        compiler_params=pltpu.CompilerParams(collective_id=1, has_side_effects=True, vmem_limit_bytes=48 << 20),
    )(share, db, wt, lead, last)

    index = lax.axis_index(("band", "chan"))
    before = jnp.where(index == 0, zero, before)
    after = jnp.where(index == group - 1, zero, after)
    pad = jnp.zeros((channels, 1), bf)
    ext_x = jnp.concatenate([pad, before[:, :W], x, after[:, :W], pad], axis=1)
    ext_g = jnp.concatenate([pad, before[:, W:], g, after[:, W:], pad], axis=1)
    column = jnp.arange(cells, dtype=jnp.int32) % W
    keep = (column != 0, None, column != W - 1)

    def window(source, a, b):
        start = 1 + a * W + b - 1
        part = lax.slice_in_dim(source, start, start + cells, axis=1)
        return part if keep[b] is None else jnp.where(keep[b][None, :], part, zero)

    conv = jnp.zeros((channels, cells), jnp.float32)
    back = jnp.zeros((channels, cells), jnp.float32)
    for a in range(3):
        for b in range(3):
            tap = kern[3 * a + b]
            conv = conv + lax.dot_general(tap, window(ext_x, a, b), (((1,), (0,)), ((), ())), preferred_element_type=jnp.float32)
            back = back + lax.dot_general(tap, window(ext_g, 2 - a, 2 - b), (((0,), (0,)), ((), ())), preferred_element_type=jnp.float32)
    outputs = (conv + bias[:, None]).astype(bf).reshape(frames.shape)
    grad_frames = back.astype(bf).reshape(frames.shape)
    grad_weight = jnp.transpose(grad.reshape(3, 3, rows_o, channels), (2, 0, 1, 3))
    return outputs, grad_frames, grad_weight, db[0]


def solution(mesh):
    cells = P(None, "clip", ("band", "chan"))
    kernel = P("chan", None, None, None)
    return jax.shard_map(
        local, mesh=mesh, in_specs=(cells, kernel, P(), cells), out_specs=(cells, cells, kernel, P("chan")), check_vma=False
    )
```

time: 258 us -> 162 us (0.63)
  the two profiles are of different devices: /device:TPU:0 before, /device:TPU:21 now
where the time goes in v1:
time: 162 us
  Pallas kernels  113 us (70%)
  matrix products  21.3 us (13%)
  local copies, waits for them, and re-layouts  18.1 us (11%)
  other arithmetic  8.45 us (5%)
    pallas_call x1, Pallas kernels, local(): pl.pallas_call(functools.partial(share_kernel, (clips, bands, chans, rows...  77.1 us
    pallas_call x1, Pallas kernels, local(): pl.pallas_call(functools.partial(gather_kernel, (bands, chans, rows_i, ro...  35.7 us
    concatenate x3, local copies, waits for them, and re-layouts, local(): sides.append(jnp.concatenate([margin, moved, margin], axis=1))  10.4 us
    dot_general x9, matrix products, local(): lax.dot_general(tap, window(ext_g, 2 - a, 2 - b), (((0,), (0,)), ((), ())...  8.9 us
    dot_general x9, matrix products, local(): lax.dot_general(tap, window(ext_x, a, b), (((1,), (0,)), ((), ())), prefe...  7.16 us
    dot_general x3, matrix products, local(): lax.dot_general(gs, window, (((1,), (1,)), ((), ())), preferred_element_t...  5.25 us
    unnamed x29, local copies, waits for them, and re-layouts  3.74 us

profile of v1, /device:TPU:21, one launch (start us, length us, event | category | flops | bytes accessed | tf_op | source)
XLA Modules:
  0.0 161.7 jit_solution(8466940978088902913)
XLA Ops:
  2.4 1.2 fusion.179
  4.0 35.7 %shard_map.75 = (bf16[128,5120]{1,0:T(8,128)(2,1)}, bf16[256,5120]{1,0:T(8,128)(2,1)}) custom-call(bf16[512,640]{1,0:T(8,128)(2,1)} %bitcast.103, bf16[512,640]{1,0:T(8,128)(2,1)} %bitcast.112), custom_call_target="tpu_custom_call" | custom-call | tf_op jit(solution)/shard_map/pallas_call | solution.py:212
  39.7 2.3 %convert_reduce_fusion = f32[256]{0:T(256)S(1)} fusion(bf16[256,5120]{1,0:T(8,128)(2,1)} %get-tuple-element.11), kind=kLoop, calls=%fused_computation | loop fusion | flops 2621184 | bytes 2622464 | tf_op jit(solution)/shard_map/reduce_sum | solution.py:237
  43.3 2.6 %concatenate.62 = bf16[128,5440]{1,0:T(8,128)(2,1)S(1)} concatenate(bf16[128,160]{1,0:T(8,128)(2,1)} %broadcast_in_dim.128, bf16[128,5120]{1,0:T(8,128)(2,1)S(1)} %copy-done.4, bf16[128,160]{1,0:T(8,128)(2,1)} %broadcast_in_dim.128), dimensions={1} | concatenate | bytes 2785280 | tf_op jit(solution)/shard_map/concatenate | solution.py:229
  46.6 1.6 %maximum_select_fusion = (bf16[128,5120]{1,0:T(8,128)(2,1)}, bf16[128,5120]{1,0:T(8,128)(2,1)S(1)}) fusion(bf16[128,5119]{1,0:T(8,128)(2,1)S(1)} %get-tuple-element.20, bf16[128,1]{1,0:T(8,128)(2,1)S(1)} %get-tuple-element.18, pred[5120]{0:T(1024)(128)(4,1)S(1)} %fusion.140, bf16[128,1]{1,0:T(8,128)(2,1)S(1)} %copy-done.7, ...), kind=kLoop, calls=%fused_computation.27 | loop fusion | flops 6553600 | bytes 5253120 | tf_op jit(solution)/shard_map/jit(_where)/select_n | solution.py:228
  48.3 4.1 %concatenate.61 = bf16[128,5440]{1,0:T(8,128)(2,1)} concatenate(bf16[128,160]{1,0:T(8,128)(2,1)} %broadcast_in_dim.128, bf16[128,5120]{1,0:T(8,128)(2,1)} %get-tuple-element.30, bf16[128,160]{1,0:T(8,128)(2,1)} %broadcast_in_dim.128), dimensions={1} | concatenate | bytes 2785280 | tf_op jit(solution)/shard_map/concatenate | solution.py:229
  52.4 3.7 %concatenate.64 = bf16[128,5440]{1,0:T(8,128)(2,1)} concatenate(bf16[128,160]{1,0:T(8,128)(2,1)} %broadcast_in_dim.128, bf16[128,5120]{1,0:T(8,128)(2,1)S(1)} %get-tuple-element.31, bf16[128,160]{1,0:T(8,128)(2,1)} %broadcast_in_dim.128), dimensions={1} | concatenate | bytes 2785280 | tf_op jit(solution)/shard_map/concatenate | solution.py:229
  56.1 2.3 %pad_maximum_fusion = bf16[384,5440]{1,0:T(8,128)(2,1)S(1)} fusion(bf16[128,5440]{1,0:T(8,128)(2,1)} %concatenate.64, bf16[128,5440]{1,0:T(8,128)(2,1)S(1)} %concatenate.62, bf16[128,5440]{1,0:T(8,128)(2,1)} %concatenate.61), kind=kLoop, calls=%fused_computation.1 | loop fusion | flops 12533760 | bytes 8355840 | tf_op jit(solution)/shard_map/concatenate | solution.py:230
  58.6 1.9 %fusion = f32[256,384]{1,0:T(8,128)S(1)} fusion(bf16[256,5120]{1,0:T(8,128)(2,1)S(1)} %copy-done.6, bf16[384,5440]{1,0:T(8,128)(2,1)S(1)} %pad_maximum_fusion), kind=kOutput, calls=%fused_computation.2 | convolution fusion | flops 1006632960 | bytes 6946816 | tf_op jit(solution)/shard_map/dot_general | solution.py:234
  60.5 1.9 %fusion.2 = f32[256,384]{1,0:T(8,128)S(1)} fusion(bf16[256,5120]{1,0:T(8,128)(2,1)S(1)} %copy-done.6, bf16[384,5440]{1,0:T(8,128)(2,1)S(1)} %pad_maximum_fusion), kind=kOutput, calls=%fused_computation.4 | convolution fusion | flops 1006632960 | bytes 6946816 | tf_op jit(solution)/shard_map/dot_general | solution.py:234
  62.4 1.5 fusion.4
  64.1 77.1 %shard_map.76 = (f32[9,256,512]{2,1,0:T(8,128)}, f32[8,256]{1,0:T(8,128)S(1)}, bf16[9,512,512]{2,1,0:T(8,128)(2,1)}, bf16[512,320]{1,0:T(8,128)(2,1)S(1)}, bf16[512,320]{1,0:T(8,128)(2,1)S(1)}) custom-call(f32[9,256,128]{2,1,0:T(8,128)S(1)} %fusion.120.s_ref, f32[8,256]{1,0:T(8,128)S(1)} %broadcast_in_dim.132.d_ref, bf16[9,256,512]{2,1,0:T(8,128)(2,1)S(1)} %bitcast.101, ...), custom_call_target="tpu_custom_call" | custom-call | tf_op jit(solution)/shard_map/pallas_call | solution.py:245
  142.9 2.2 %fusion.21 = f32[512,640]{1,0:T(8,128)S(1)} fusion(bf16[512,1]{1,0:T(8,128)(2,1)S(1)} %broadcast_in_dim.134, bf16[512,160]{1,0:T(8,128)(2,1)S(1)} %get-tuple-element.28, bf16[512,640]{1,0:T(8,128)(2,1)S(1)} %bitcast.114, pred[640]{0:T(1024)(128)(4,1)S(1)} %copy-done.9, bf16[9,512,512]{2,1,0:T(8,128)(2,1)} %get-tuple-element.13), kind=kOutput, calls=%fused_computation.58 | convolution fusion | flops 337838080 | bytes 2655872 | tf_op jit(solution)/shard_map/dot_general | solution.py:284
  145.2 0.7 convolution_add_fusion.7
  146.0 0.7 convolution_add_fusion.6
  146.7 0.8 convolution_add_fusion.5
  148.1 0.8 convolution_add_fusion.3
  148.9 0.8 convolution_add_fusion.2
  150.3 1.6 fusion.9
  151.9 0.7 fusion.13
  154.1 0.7 convolution_add_fusion.13
  156.1 0.7 convolution_add_fusion.10
  157.9 1.5 fusion.10
  159.5 2.2 %copy.17 = f32[256,3,3,512]{3,0,2,1:T(8,128)} copy(f32[256,3,3,512]{3,0,2,1:T(8,128)S(1)} %bitcast.124) | data formatting | bytes 9437184
  (62 shorter events, 11.3 us)
Async XLA Ops:
  0.6 2.9 %copy-start.2 = (bf16[512,1,640]{2,0,1:T(8,128)(2,1)S(1)}, bf16[512,1,640]{2,0,1:T(8,128)(2,1)}, u32[]{:S(2)}) copy-start(bf16[512,1,640]{2,0,1:T(8,128)(2,1)} %param.7) | copy-start | bytes 1966084
  39.7 2.3 %copy-start.4 = (bf16[128,5120]{1,0:T(8,128)(2,1)S(1)}, bf16[128,5120]{1,0:T(8,128)(2,1)}, u32[]{:S(2)}) copy-start(bf16[128,5120]{1,0:T(8,128)(2,1)} %get-tuple-element.12) | copy-start | bytes 3932164
  45.9 0.8 copy-start.7
  45.9 0.8 copy-start.8
  56.1 2.6 %copy-start.6 = (bf16[256,5120]{1,0:T(8,128)(2,1)S(1)}, bf16[256,5120]{1,0:T(8,128)(2,1)}, u32[]{:S(2)}) copy-start(bf16[256,5120]{1,0:T(8,128)(2,1)} %get-tuple-element.11) | copy-start | bytes 7864324
  62.4 1.8 %copy-start = (bf16[256,3,3,512]{3,0,2,1:T(8,128)(2,1)S(1)}, bf16[256,3,3,512]{3,0,2,1:T(8,128)(2,1)}, u32[]{:S(2)}) copy-start(bf16[256,3,3,512]{3,0,2,1:T(8,128)(2,1)} %param.5) | copy-start | bytes 7077892
  141.8 1.1 copy-start.3
  141.8 1.1 copy-start.9
  142.0 3.1 %copy-start.5 = (bf16[9,512,512]{2,1,0:T(8,128)(2,1)S(1)}, bf16[9,512,512]{2,1,0:T(8,128)(2,1)}, u32[]{:S(2)}) copy-start(bf16[9,512,512]{2,1,0:T(8,128)(2,1)} %get-tuple-element.13) | copy-start | bytes 14155780
  145.2 0.8 copy-start.10
  150.3 1.6 %copy-start.1 = (bf16[512,1,640]{2,0,1:T(8,128)(2,1)S(1)}, bf16[512,1,640]{2,0,1:T(8,128)(2,1)}, u32[]{:S(2)}) copy-start(bf16[512,1,640]{2,0,1:T(8,128)(2,1)} %param.4) | copy-start | bytes 1966084
  156.1 3.4 %slice-start = ((s8[4718592]{0:T(1024)(128)(4,1)}), s8[4194304]{0:T(1024)(128)(4,1)S(1)}, s32[]{:S(2)}) async-start(s8[4718592]{0:T(1024)(128)(4,1)} %bitcast.122), calls=%async_computation | async-start | bytes 8388608
  156.9 1.1 copy-start.11
  156.9 2.6 %slice-start.1 = ((s8[4718592]{0:T(1024)(128)(4,1)}), s8[524288]{0:T(1024)(128)(4,1)S(1)}, s32[]{:S(2)}) async-start(s8[4718592]{0:T(1024)(128)(4,1)} %bitcast.122), calls=%async_computation.1 | async-start | bytes 1048576

commit v2 on v0

v2 whole, which is shorter than its diff:
```python
import functools
import math

import jax
import jax.numpy as jnp
from jax import lax
from jax.experimental import pallas as pl
from jax.experimental.pallas import tpu as pltpu
from jax.sharding import PartitionSpec as P

W = 160
MESH = pl.DeviceIdType.MESH
F32 = jnp.float32
BF16 = jnp.bfloat16


def ds(start, size):
    return pl.ds(pl.multiple_of(start, size), size)


def remote(src, dst, send, recv, device):
    return pltpu.make_async_remote_copy(
        src_ref=src, dst_ref=dst, send_sem=send, recv_sem=recv, device_id=device, device_id_type=MESH
    )


def sides(rows):
    wide = rows.astype(F32)
    at = lax.broadcasted_iota(jnp.int32, wide.shape, 0)
    left = jnp.where(at == 0, 0.0, pltpu.roll(wide, 1, 0)).astype(BF16)
    right = jnp.where(at == W - 1, 0.0, pltpu.roll(wide, W - 1, 0)).astype(BF16)
    return left, rows, right


def kernel(
    dims, xt_ref, gt_ref, g_ref, w_ref, bias_ref, o_ref, db_ref, out_ref, back_ref,
    xs, gs, dx, xe, ge, kern, acc, share, got1, got2, dbs, dgot, hx, hg, sems, regs,
):
    clips, bands, chans, rows_o, rows_i, cells, channels, scale = dims
    group = bands * chans
    half = rows_o // 2
    lanes = channels // clips
    width = bands // 2
    units = cells // W
    total = cells * group
    z, b, n = lax.axis_index("clip"), lax.axis_index("band"), lax.axis_index("chan")
    me = b * chans + n
    core = b % 2
    sib = b + 1 - 2 * core
    sib_id = {"band": sib}
    nxt, prv = (me + 1) % group, (me + group - 1) % group
    nxt_id = {"band": nxt // chans, "chan": nxt % chans}
    prv_id = {"band": prv // chans, "chan": prv % chans}
    z0, z1 = z % 2, z // 2
    near, far = {"clip": z + 1 - 2 * z0}, {"clip": (z + 2) % clips}

    barrier = pltpu.get_barrier_semaphore()
    targets = [{"clip": (z + k) % clips} for k in range(1, clips)]
    for k in range(1, group):
        to = (me + k) % group
        targets.append({"band": to // chans, "chan": to % chans})
    for target in targets:
        pl.semaphore_signal(barrier, inc=1, device_id=target, device_id_type=MESH)
    pl.semaphore_wait(barrier, len(targets))

    started = []
    names = {}

    def pair(key):
        if key not in names:
            names[key] = len(names)
        return sems.at[0, names[key]], sems.at[1, names[key]]

    def send(src, dst, key, device):
        s, r = pair(key)
        copy = remote(src, dst, s, r, device)
        copy.start()
        started.append(copy)

    def arrive(dst, key):
        s, r = pair(key)
        remote(dst, dst, s, r, sib_id).wait_recv()

    def slab(src_n, part, zz):
        return kern.at[:, ds((2 * src_n + part) * half, half), ds(zz * lanes, lanes)]

    for m in range(1, chans):
        send(w_ref.at[:, ds(core * half, half), ds(z * lanes, lanes)], slab(n, core, z), ("w", m), {"chan": (n + m) % chans})
    keep_w = pltpu.make_async_copy(w_ref, kern.at[:, ds(n * rows_o, rows_o), :], regs.at[0])
    keep_w.start()
    keep_x = pltpu.make_async_copy(xt_ref.at[:, ds(b * rows_i, rows_i)], xs.at[ds(me * cells, cells), :], regs.at[1])
    keep_g = pltpu.make_async_copy(g_ref.at[ds(n * rows_o, rows_o), :], gs.at[:, ds(me * cells, cells)], regs.at[2])
    keep_x.start()
    keep_g.start()

    pairs = [(j, m) for j in range(width) for m in range(chans)]
    for j, m in pairs[1:]:
        to_b, to_n = (b + 2 * j) % bands, (n + m) % chans
        send(
            g_ref.at[ds(to_n * rows_o, rows_o), :], gs.at[:, ds(me * cells, cells)], ("g", j, m),
            {"band": to_b, "chan": to_n},
        )
    for k in range(1, group):
        to = (me + k) % group
        to_b, to_n = to // chans, to % chans
        send(
            xt_ref.at[:, ds(to_b * rows_i, rows_i)], xs.at[ds(me * cells, cells), :], ("x", k),
            {"band": to_b, "chan": to_n},
        )
    send(g_ref.at[ds(n * rows_o, rows_o), :], gs.at[:, ds(me * cells, cells)], ("f", 0, 0), sib_id)
    send(xt_ref.at[pl.ds(cells - W, W), :], hx.at[0], ("hx", 0), nxt_id)
    send(gt_ref.at[pl.ds(cells - W, W), :], hg.at[0], ("hg", 0), nxt_id)
    send(xt_ref.at[pl.ds(0, W), :], hx.at[1], ("hx", 1), prv_id)
    send(gt_ref.at[pl.ds(0, W), :], hg.at[1], ("hg", 1), prv_id)

    for m in range(1, chans):
        src = (n + chans - m) % chans
        arrive(slab(src, core, z), ("w", m))
        for q in range(1, clips):
            send(slab(src, core, z), slab(src, core, z), ("wz", m, q), {"clip": (z + q) % clips})
        send(slab(src, core, z), slab(src, core, z), ("ws", m, 0), sib_id)

    def widen(dst, to, rows, size):
        for t, part in enumerate(sides(rows)):
            dst[ds(to, W), t * size:(t + 1) * size] = part

    @pl.loop(0, units)
    def _(u):
        widen(xe, (u + 1) * W, xt_ref[ds(u * W, W), :], channels)
        widen(ge, (u + 1) * W, gt_ref[ds(u * W, W), :], channels)

    for j, m in pairs[1:]:
        src = ((b + bands - 2 * j) % bands) * chans + (n + chans - m) % chans
        place = gs.at[:, ds(src * cells, cells)]
        arrive(place, ("g", j, m))
        send(place, place, ("f", j, m), sib_id)
    for k in range(1, group):
        src = (me + group - k) % group
        arrive(xs.at[ds(src * cells, cells), :], ("x", k))
    keep_x.wait()
    dx[pl.ds(0, W), :] = jnp.zeros((W, 3 * rows_i), BF16)
    dx[pl.ds(total + W, W), :] = jnp.zeros((W, 3 * rows_i), BF16)

    @pl.loop(0, total // W)
    def _(u):
        widen(dx, (u + 1) * W, xs[ds(u * W, W), :], rows_i)

    for j, m in pairs:
        src = ((sib + bands - 2 * j) % bands) * chans + (n + chans - m) % chans
        arrive(gs.at[:, ds(src * cells, cells)], ("f", j, m))
    keep_g.wait()

    block = 2 * cells

    def tap_row(a):
        acc2 = acc.at[pl.ds(0, rows_o), pl.ds(0, 3 * rows_i)]
        acc2[...] = jnp.zeros((rows_o, 3 * rows_i), F32)

        @pl.loop(0, group // 2)
        def _(k):
            rows = pl.ds(pl.multiple_of(k * block + a * W, 32), block)
            acc2[...] += jnp.dot(gs[:, ds(k * block, block)], dx[rows, :], preferred_element_type=F32)

        for t in range(3):
            share[3 * a + t] = acc2[:, t * rows_i:(t + 1) * rows_i] * scale
        taps = pl.ds(3 * a, 3)
        send(share.at[taps, ds((1 - z0) * half, half), :], got1.at[taps], ("r1", a), near)

    quarter = half // 2

    def spot(a, start, size, bb):
        return o_ref.at[pl.ds(3 * a, 3), ds(start, size), ds(bb * rows_i, rows_i)]

    def reduce1(a):
        arrive(got1.at[pl.ds(3 * a, 3)], ("r1", a))
        for t in range(3 * a, 3 * a + 3):
            share[t, ds(z0 * half, half), :] += got1[t]
        send(
            share.at[pl.ds(3 * a, 3), ds((2 * z0 + 1 - z1) * quarter, quarter), :],
            got2.at[pl.ds(3 * a, 3)], ("r2", a), far,
        )

    def spread(a, start, size, step):
        place = spot(a, start, size, b)
        for j in range(1, width):
            send(place, place, ("xo", a, step, j), {"band": (b + 2 * j) % bands})
        send(place, place, ("c", a, step, 0), sib_id)

    mine = (2 * z0 + z1) * quarter
    other = (2 * z0 + 1 - z1) * quarter

    def reduce2(a):
        arrive(got2.at[pl.ds(3 * a, 3)], ("r2", a))
        for t in range(3 * a, 3 * a + 3):
            o_ref[t, ds(mine, quarter), ds(b * rows_i, rows_i)] = share[t, ds(mine, quarter), :] + got2[t]
        send(spot(a, mine, quarter, b), spot(a, mine, quarter, b), ("a1", a), far)
        spread(a, mine, quarter, 0)

    def gather1(a):
        arrive(spot(a, other, quarter, b), ("a1", a))
        send(spot(a, z0 * half, half, b), spot(a, z0 * half, half, b), ("a2", a), near)
        spread(a, other, quarter, 1)

    def gather2(a):
        arrive(spot(a, (1 - z0) * half, half, b), ("a2", a))
        spread(a, (1 - z0) * half, half, 2)

    def regions(step):
        return ((mine, quarter), (other, quarter), ((1 - z0) * half, half))[step]

    def cross(a):
        for step in range(3):
            start, size = regions(step)
            for j in range(1, width):
                place = spot(a, start, size, (b + bands - 2 * j) % bands)
                arrive(place, ("xo", a, step, j))
                send(place, place, ("c", a, step, j), sib_id)

    def finish(a):
        for step in range(3):
            start, size = regions(step)
            for j in range(width):
                arrive(spot(a, start, size, (sib + bands - 2 * j) % bands), ("c", a, step, j))

    def conv(a):
        @pl.loop(0, channels // 256)
        def _(t):
            rows = ds(t * 256, 256)
            part = jnp.zeros((256, cells), F32) + bias_ref[rows, :] if a == 0 else acc[rows, :]
            for s in range(3):
                part += lax.dot_general(
                    kern[3 * a + s, rows, :], xe[a * W:a * W + cells, s * channels:(s + 1) * channels],
                    (((1,), (1,)), ((), ())), preferred_element_type=F32,
                )
            if a == 2:
                out_ref[rows, :] = part.astype(BF16)
            else:
                acc[rows, :] = part

    half_cells = cells // 2

    def back(a):
        @pl.loop(0, 2)
        def _(t):
            rows = ds(t * half_cells, half_cells)
            c = 2 - a
            part = jnp.zeros((half_cells, channels), F32)
            if a:
                part = acc[ds(t * half_cells, half_cells), pl.ds(0, channels)]
            for s in range(3):
                part += jnp.dot(
                    ge[pl.ds(pl.multiple_of(c * W + t * half_cells, 32), half_cells), (2 - s) * channels:(3 - s) * channels],
                    kern[3 * a + s], preferred_element_type=F32,
                )
            if a == 2:
                back_ref[rows, :] = part.astype(BF16)
            else:
                acc[rows, pl.ds(0, channels)] = part

    def bias_sum():
        ones = jnp.ones((8, block), BF16)
        dbs[...] = jnp.zeros((8, rows_o), F32)

        @pl.loop(0, group // 2)
        def _(k):
            dbs[...] += lax.dot_general(
                ones, gs[:, ds(k * block, block)], (((1,), (1,)), ((), ())), preferred_element_type=F32
            )

        for q in range(1, clips):
            send(dbs, dgot.at[q], ("d", q), {"clip": (z + q) % clips})

    def halos():
        for h in range(2):
            arrive(hx.at[h], ("hx", h))
            arrive(hg.at[h], ("hg", h))
            edge = me == (0 if h == 0 else group - 1)
            for src, dst in ((hx, xe), (hg, ge)):
                rows = src[h]
                rows = jnp.where(edge, jnp.zeros_like(rows), rows)
                for t, part in enumerate(sides(rows)):
                    dst[pl.ds(h * (cells + W), W), t * channels:(t + 1) * channels] = part

    def weights():
        for m in range(1, chans):
            src = (n + chans - m) % chans
            for q in range(1, clips):
                zz = (z + clips - q) % clips
                arrive(slab(src, core, zz), ("wz", m, q))
                send(slab(src, core, zz), slab(src, core, zz), ("ws", m, q), sib_id)
        for m in range(1, chans):
            src = (n + chans - m) % chans
            for q in range(clips):
                arrive(slab(src, 1 - core, (z + clips - q) % clips), ("ws", m, q))
        keep_w.wait()

    tap_row(0)
    tap_row(1)
    reduce1(0)
    tap_row(2)
    bias_sum()
    reduce1(1)
    halos()
    reduce2(0)
    reduce1(2)
    weights()
    conv(0)
    reduce2(1)
    gather1(0)
    conv(1)
    reduce2(2)
    gather1(1)
    conv(2)
    gather2(0)
    gather1(2)
    back(0)
    gather2(1)
    cross(0)
    back(1)
    gather2(2)
    cross(1)
    back(2)
    cross(2)
    for q in range(1, clips):
        arrive(dgot.at[q], ("d", q))
    sums = dbs[...]
    for q in range(1, clips):
        sums = sums + dgot[q]
    db_ref[...] = sums * scale
    for a in range(3):
        finish(a)
    for copy in started:
        copy.wait_send()


VM = pl.BlockSpec(memory_space=pltpu.VMEM)


def local(frames, weight, bias, cotangent):
    channels, frame_count, cells = frames.shape
    clips, bands, chans = (lax.axis_size(a) for a in ("clip", "band", "chan"))
    group = bands * chans
    assert frame_count == 1 and cells % W == 0 and clips == 4
    total = cells * group
    scale = 1.0 / math.sqrt(frame_count * clips * total)
    rows_i, rows_o = channels // bands, channels // chans
    x = frames.reshape(channels, cells)
    g = cotangent.reshape(channels, cells)
    wt = jnp.transpose(weight, (1, 2, 0, 3)).reshape(9, rows_o, channels)
    half = rows_o // 2
    width = bands // 2
    copies = (chans - 1) * (1 + clips - 1 + clips) + 2 * width * chans + group + 4 + 12 + clips + 9 * (2 * width) + 8
    shape = jax.ShapeDtypeStruct
    grad, db, outputs, back = pl.pallas_call(
        functools.partial(kernel, (clips, bands, chans, rows_o, rows_i, cells, channels, scale)),
        out_shape=(
            shape((9, rows_o, channels), F32),
            shape((8, rows_o), F32),
            shape((channels, cells), BF16),
            shape((cells, channels), BF16),
        ),
        in_specs=[VM] * 5,
        out_specs=(VM,) * 4,
        scratch_shapes=[
            pltpu.VMEM((total, rows_i), BF16),
            pltpu.VMEM((rows_o, total), BF16),
            pltpu.VMEM((total + 2 * W, 3 * rows_i), BF16),
            pltpu.VMEM((cells + 2 * W, 3 * channels), BF16),
            pltpu.VMEM((cells + 2 * W, 3 * channels), BF16),
            pltpu.VMEM((9, channels, channels), BF16),
            pltpu.VMEM((max(channels, cells), max(channels, cells)), F32),
            pltpu.VMEM((9, rows_o, rows_i), F32),
            pltpu.VMEM((9, half, rows_i), F32),
            pltpu.VMEM((9, half // 2, rows_i), F32),
            pltpu.VMEM((8, rows_o), F32),
            pltpu.VMEM((clips, 8, rows_o), F32),
            pltpu.VMEM((2, W, channels), BF16),
            pltpu.VMEM((2, W, channels), BF16),
            pltpu.SemaphoreType.DMA((2, copies)),
            pltpu.SemaphoreType.DMA((3,)),
        ],
        compiler_params=pltpu.CompilerParams(collective_id=0, has_side_effects=True, vmem_limit_bytes=67000000),
    )(x.T, g.T, g, wt, bias[:, None])
    outputs = outputs.reshape(frames.shape)
    grad_frames = back.T.reshape(frames.shape)
    grad_weight = jnp.transpose(grad.reshape(3, 3, rows_o, channels), (2, 0, 1, 3))
    return outputs, grad_frames, grad_weight, db[0]


def solution(mesh):
    cells = P(None, "clip", ("band", "chan"))
    taps = P("chan", None, None, None)
    return jax.shard_map(
        local, mesh=mesh, in_specs=(cells, taps, P(), cells), out_specs=(cells, cells, taps, P("chan")), check_vma=False
    )
```

time: 258 us -> 124 us (0.48)
  waiting for transfers between devices: 157 us -> 0 us
  Pallas kernels: 0 us -> 107 us
  blocking collectives: 31 us -> 0 us
  matrix products: 27.1 us -> 0 us
  between operations: 17.1 us -> 0.64 us
  starting transfers between devices: 7 us -> 0 us
  other arithmetic: 4.74 us -> 0 us
    pallas_call x0 -> x1, Pallas kernels: none -> 107 us  [local(): pl.pallas_call(functools.partial(kernel, (clips, bands, chans, rows_o, ro...]
    reduce_scatter x1 -> x0, waiting for transfers between devices: 82.1 us -> none  [local(): lax.psum_scatter(dw_order, ('band', 'chan'), scatter_dimension=0, tiled=T...]
    psum x1 -> x0, waiting for transfers between devices: 57.7 us -> none  [local(): dw_share, db_share = lax.psum((dw_share, db_share), 'clip')]
    dot_general x27 -> x0, matrix products: 27.1 us -> none  [the longest x9 10.6 us: local(): jnp.einsum('ofs,oi->ifs', cot_windows[3 * a + b], kernel[:, a, b, :], pre...]
    unnamed x2 -> x0, blocking collectives: 20.8 us -> none
    ppermute x2 -> x0, waiting for transfers between devices: 16.6 us -> none  [the longest x1 10.1 us: padded(): after = lax.ppermute(leading, axis, down)]
    psum x1 -> x0, blocking collectives: 10.2 us -> none  [local(): dw_share, db_share = lax.psum((dw_share, db_share), 'clip')]
    ppermute x2 -> x0, starting transfers between devices: 6.84 us -> none  [the longest x1 5.56 us: padded(): before = lax.ppermute(last, axis, up)]
  transfers between devices with their start and end apart: 6 -> 0, of which waited for: 4 -> 0; matrix products, arithmetic and copies ran while one was open for 10% -> 0% of each run, Pallas kernels for 0% -> 0%
where the time goes in v2:
time: 124 us; the launch traced here: 123 us
  Pallas kernels  107 us (86%)
  local copies, waits for them, and re-layouts  16.3 us (13%)
    pallas_call x1, Pallas kernels, local(): pl.pallas_call(functools.partial(kernel, (clips, bands, chans, rows_o, ro...  107 us
    unnamed x4, local copies, waits for them, and re-layouts  11.3 us

profile of v2, /device:TPU:0, one launch (start us, length us, event | category | flops | bytes accessed | tf_op | source)
XLA Modules:
  0.0 123.5 jit_solution(6655479164325739323)
XLA Ops:
  0.6 1.5 %copy.13.bias_ref = f32[512,1]{1,0:T(8,128)} copy(f32[512,1]{0,1:T(1,128)} %bitcast.25) | data formatting | bytes 4096 | tf_op jit(solution)/shard_map/broadcast_in_dim | solution.py:383
  2.2 2.2 %copy.11 = bf16[512,1,640]{0,2,1:T(8,128)(2,1)} copy(bf16[512,1,640]{2,0,1:T(8,128)(2,1)} %param.4) | data formatting | bytes 1310720 | tf_op args[0]
  4.3 2.2 %copy.12.gt_ref = bf16[640,512]{1,0:T(8,128)(2,1)} copy(bf16[640,512]{0,1:T(8,128)(2,1)} %bitcast.19) | data formatting | bytes 1310720 | tf_op jit(solution)/shard_map/transpose | solution.py:383
  6.5 106.5 %shard_map.75 = (f32[9,256,512]{2,1,0:T(8,128)}, f32[8,256]{1,0:T(8,128)}, bf16[512,640]{1,0:T(8,128)(2,1)}, bf16[640,512]{1,0:T(8,128)(2,1)}) custom-call(bf16[640,512]{1,0:T(8,128)(2,1)} %bitcast.21, bf16[640,512]{1,0:T(8,128)(2,1)} %copy.12.gt_ref, bf16[512,640]{1,0:T(8,128)(2,1)} %bitcast.20, bf16[9,256,512]{2,1,0:T(8,128)(2,1)} %bitcast.22, ...), custom_call_target="tpu_custom_call" | custom-call | tf_op jit(solution)/shard_map/pallas_call | solution.py:354
  113.0 2.2 %copy.14 = bf16[512,1,640]{2,0,1:T(8,128)(2,1)} copy(bf16[512,1,640]{0,2,1:T(8,128)(2,1)} %bitcast.24) | data formatting | bytes 1310720
  115.2 1.3 %slice.3 = f32[1,256]{1,0:T(1,128)} slice(f32[8,256]{1,0:T(8,128)} %get-tuple-element.11), slice={[0:1], [0:256]} | slice | bytes 2048 | tf_op jit(solution)/shard_map/slice | solution.py:387
  116.5 2.0 %copy.17 = bf16[512,1,640]{2,0,1:T(8,128)(2,1)} copy(bf16[512,1,640]{2,0,1:T(8,128)(2,1)} %bitcast.23) | data formatting | bytes 1310720
  118.5 5.0 %copy.18 = f32[256,3,3,512]{3,0,2,1:T(8,128)} copy(f32[256,3,3,512]{3,0,2,1:T(8,128)} %bitcast.18) | data formatting | bytes 9437184

commit v3 on v2

--- a/solution.py
+++ b/solution.py
@@ -33,8 +33,8 @@
 
 
 def kernel(
-    dims, xt_ref, gt_ref, g_ref, w_ref, bias_ref, o_ref, db_ref, out_ref, back_ref,
-    xs, gs, dx, xe, ge, kern, acc, share, got1, got2, dbs, dgot, hx, hg, sems, regs,
+    dims, x_ref, g_ref, w_ref, bias_ref, o_ref, db_ref, out_ref, back_ref,
+    xs, gs, dx, xe, ge, kern, acc, share, got1, got2, dbs, dgot, hx, hg, xt_ref, gt_ref, sems, regs,
 ):
     clips, bands, chans, rows_o, rows_i, cells, channels, scale = dims
     group = bands * chans
@@ -61,6 +61,13 @@
         targets.append({"band": to // chans, "chan": to % chans})
     for target in targets:
         pl.semaphore_signal(barrier, inc=1, device_id=target, device_id_type=MESH)
+
+    def turn(src, dst):
+        @pl.loop(0, cells // 128)
+        def _(t):
+            dst[ds(t * 128, 128), :] = src[:, ds(t * 128, 128)].astype(F32).T.astype(BF16)
+
+    turn(x_ref, xt_ref)
     pl.semaphore_wait(barrier, len(targets))
 
     started = []
@@ -84,70 +91,99 @@
     def slab(src_n, part, zz):
         return kern.at[:, ds((2 * src_n + part) * half, half), ds(zz * lanes, lanes)]
 
+    keep_w = pltpu.make_async_copy(w_ref, kern.at[:, ds(n * rows_o, rows_o), :], regs.at[0])
+    keep_x = pltpu.make_async_copy(xt_ref.at[:, ds(b * rows_i, rows_i)], xs.at[ds(me * cells, cells), :], regs.at[1])
+    keep_g = pltpu.make_async_copy(g_ref.at[ds(n * rows_o, rows_o), :], gs.at[:, ds(me * cells, cells)], regs.at[2])
+
+    def x_place(src_b, src_n):
+        return xs.at[ds((src_b * chans + src_n) * cells, cells), :]
+
+    def g_place(src_b, src_n):
+        return gs.at[:, ds((src_b * chans + src_n) * cells, cells)]
+
+    for d in range(1, bands):
+        to_b = (b + d) % bands
+        send(xt_ref.at[:, ds(to_b * rows_i, rows_i)], x_place(b, n), ("x", d, 0), {"band": to_b})
+    for m in range(1, chans):
+        to_n = (n + m) % chans
+        send(g_ref.at[ds(to_n * rows_o, rows_o), :], g_place(b, n), ("g", 0, m), {"chan": to_n})
+        send(xt_ref.at[:, ds(b * rows_i, rows_i)], x_place(b, n), ("x", 0, m), {"chan": to_n})
     for m in range(1, chans):
         send(w_ref.at[:, ds(core * half, half), ds(z * lanes, lanes)], slab(n, core, z), ("w", m), {"chan": (n + m) % chans})
-    keep_w = pltpu.make_async_copy(w_ref, kern.at[:, ds(n * rows_o, rows_o), :], regs.at[0])
-    keep_w.start()
-    keep_x = pltpu.make_async_copy(xt_ref.at[:, ds(b * rows_i, rows_i)], xs.at[ds(me * cells, cells), :], regs.at[1])
-    keep_g = pltpu.make_async_copy(g_ref.at[ds(n * rows_o, rows_o), :], gs.at[:, ds(me * cells, cells)], regs.at[2])
+    own_g = g_ref.at[ds(n * rows_o, rows_o), :]
+    for j in range(1, width):
+        send(own_g, g_place(b, n), ("g", j, 0), {"band": (b + 2 * j) % bands})
+    send(own_g, g_place(b, n), ("f", 0, 0), sib_id)
     keep_x.start()
     keep_g.start()
-
-    pairs = [(j, m) for j in range(width) for m in range(chans)]
-    for j, m in pairs[1:]:
-        to_b, to_n = (b + 2 * j) % bands, (n + m) % chans
-        send(
-            g_ref.at[ds(to_n * rows_o, rows_o), :], gs.at[:, ds(me * cells, cells)], ("g", j, m),
-            {"band": to_b, "chan": to_n},
-        )
-    for k in range(1, group):
-        to = (me + k) % group
-        to_b, to_n = to // chans, to % chans
-        send(
-            xt_ref.at[:, ds(to_b * rows_i, rows_i)], xs.at[ds(me * cells, cells), :], ("x", k),
-            {"band": to_b, "chan": to_n},
-        )
-    send(g_ref.at[ds(n * rows_o, rows_o), :], gs.at[:, ds(me * cells, cells)], ("f", 0, 0), sib_id)
-    send(xt_ref.at[pl.ds(cells - W, W), :], hx.at[0], ("hx", 0), nxt_id)
-    send(gt_ref.at[pl.ds(cells - W, W), :], hg.at[0], ("hg", 0), nxt_id)
-    send(xt_ref.at[pl.ds(0, W), :], hx.at[1], ("hx", 1), prv_id)
-    send(gt_ref.at[pl.ds(0, W), :], hg.at[1], ("hg", 1), prv_id)
-
+    keep_w.start()
+
+    def widen(dst, to, rows, size):
+        for t, part in enumerate(sides(rows)):
+            dst[ds(to, W), t * size:(t + 1) * size] = part
+
+    def widen_block(src):
+        @pl.loop(0, units)
+        def _(u):
+            at = src * cells + u * W
+            widen(dx, at + W, xs[ds(at, W), :], rows_i)
+
+    for d in range(1, bands):
+        place = x_place((b + bands - d) % bands, n)
+        arrive(place, ("x", d, 0))
+        for m in range(1, chans):
+            send(place, place, ("x", d, m), {"chan": (n + m) % chans})
+    for m in range(1, chans):
+        place = g_place(b, (n + chans - m) % chans)
+        arrive(place, ("g", 0, m))
+        for j in range(1, width):
+            send(place, place, ("g", j, m), {"band": (b + 2 * j) % bands})
+        send(place, place, ("f", 0, m), sib_id)
     for m in range(1, chans):
         src = (n + chans - m) % chans
         arrive(slab(src, core, z), ("w", m))
         for q in range(1, clips):
             send(slab(src, core, z), slab(src, core, z), ("wz", m, q), {"clip": (z + q) % clips})
         send(slab(src, core, z), slab(src, core, z), ("ws", m, 0), sib_id)
-
-    def widen(dst, to, rows, size):
-        for t, part in enumerate(sides(rows)):
-            dst[ds(to, W), t * size:(t + 1) * size] = part
+    for j in range(1, width):
+        place = g_place((b + bands - 2 * j) % bands, n)
+        arrive(place, ("g", j, 0))
+        send(place, place, ("f", j, 0), sib_id)
+
+    turn(g_ref, gt_ref)
+    dx[pl.ds(0, W), :] = jnp.zeros((W, 3 * rows_i), BF16)
+    dx[pl.ds(total + W, W), :] = jnp.zeros((W, 3 * rows_i), BF16)
 
     @pl.loop(0, units)
     def _(u):
         widen(xe, (u + 1) * W, xt_ref[ds(u * W, W), :], channels)
         widen(ge, (u + 1) * W, gt_ref[ds(u * W, W), :], channels)
 
-    for j, m in pairs[1:]:
-        src = ((b + bands - 2 * j) % bands) * chans + (n + chans - m) % chans
-        place = gs.at[:, ds(src * cells, cells)]
-        arrive(place, ("g", j, m))
-        send(place, place, ("f", j, m), sib_id)
-    for k in range(1, group):
-        src = (me + group - k) % group
-        arrive(xs.at[ds(src * cells, cells), :], ("x", k))
     keep_x.wait()
-    dx[pl.ds(0, W), :] = jnp.zeros((W, 3 * rows_i), BF16)
-    dx[pl.ds(total + W, W), :] = jnp.zeros((W, 3 * rows_i), BF16)
-
-    @pl.loop(0, total // W)
-    def _(u):
-        widen(dx, (u + 1) * W, xs[ds(u * W, W), :], rows_i)
-
-    for j, m in pairs:
-        src = ((sib + bands - 2 * j) % bands) * chans + (n + chans - m) % chans
-        arrive(gs.at[:, ds(src * cells, cells)], ("f", j, m))
+    widen_block(me)
+    for d in range(1, bands):
+        widen_block(((b + bands - d) % bands) * chans + n)
+    for m in range(1, chans):
+        src_n = (n + chans - m) % chans
+        arrive(x_place(b, src_n), ("x", 0, m))
+        widen_block(b * chans + src_n)
+    for j in range(1, width):
+        for m in range(1, chans):
+            place = g_place((b + bands - 2 * j) % bands, (n + chans - m) % chans)
+            arrive(place, ("g", j, m))
+            send(place, place, ("f", j, m), sib_id)
+    for d in range(1, bands):
+        for m in range(1, chans):
+            src_b, src_n = (b + bands - d) % bands, (n + chans - m) % chans
+            arrive(x_place(src_b, src_n), ("x", d, m))
+            widen_block(src_b * chans + src_n)
+    send(xt_ref.at[pl.ds(cells - W, W), :], hx.at[0], ("hx", 0), nxt_id)
+    send(gt_ref.at[pl.ds(cells - W, W), :], hg.at[0], ("hg", 0), nxt_id)
+    send(xt_ref.at[pl.ds(0, W), :], hx.at[1], ("hx", 1), prv_id)
+    send(gt_ref.at[pl.ds(0, W), :], hg.at[1], ("hg", 1), prv_id)
+    for j in range(width):
+        for m in range(chans):
+            arrive(g_place((sib + bands - 2 * j) % bands, (n + chans - m) % chans), ("f", j, m))
     keep_g.wait()
 
     block = 2 * cells
@@ -226,7 +262,11 @@
         @pl.loop(0, channels // 256)
         def _(t):
             rows = ds(t * 256, 256)
-            part = jnp.zeros((256, cells), F32) + bias_ref[rows, :] if a == 0 else acc[rows, :]
+            if a == 0:
+                column = jnp.broadcast_to(bias_ref[:, rows], (8, 256)).T[:, :1]
+                part = jnp.zeros((256, cells), F32) + column
+            else:
+                part = acc[rows, :]
             for s in range(3):
                 part += lax.dot_general(
                     kern[3 * a + s, rows, :], xe[a * W:a * W + cells, s * channels:(s + 1) * channels],
@@ -252,10 +292,12 @@
                     ge[pl.ds(pl.multiple_of(c * W + t * half_cells, 32), half_cells), (2 - s) * channels:(3 - s) * channels],
                     kern[3 * a + s], preferred_element_type=F32,
                 )
-            if a == 2:
-                back_ref[rows, :] = part.astype(BF16)
-            else:
-                acc[rows, pl.ds(0, channels)] = part
+            acc[rows, pl.ds(0, channels)] = part
+
+        if a == 2:
+            @pl.loop(0, cells // 128)
+            def _(t):
+                back_ref[:, ds(t * 128, 128)] = acc[ds(t * 128, 128), pl.ds(0, channels)].T.astype(BF16)
 
     def bias_sum():
         ones = jnp.ones((8, block), BF16)
@@ -326,11 +368,20 @@
     sums = dbs[...]
     for q in range(1, clips):
         sums = sums + dgot[q]
-    db_ref[...] = sums * scale
+    db_ref[...] = sums[:1] * scale
     for a in range(3):
         finish(a)
     for copy in started:
         copy.wait_send()
+
+
+def emit(*refs):
+    sources, places, sems = refs[:4], refs[4:8], refs[8]
+    copies = [pltpu.make_async_copy(src, dst, sems.at[i]) for i, (src, dst) in enumerate(zip(sources, places))]
+    for copy in copies:
+        copy.start()
+    for copy in copies:
+        copy.wait()
 
 
 VM = pl.BlockSpec(memory_space=pltpu.VMEM)
@@ -349,17 +400,18 @@
     wt = jnp.transpose(weight, (1, 2, 0, 3)).reshape(9, rows_o, channels)
     half = rows_o // 2
     width = bands // 2
-    copies = (chans - 1) * (1 + clips - 1 + clips) + 2 * width * chans + group + 4 + 12 + clips + 9 * (2 * width) + 8
+    copies = (chans - 1) * (1 + clips - 1 + clips) + 2 * width * chans + group + bands * chans + 4 + 12 + clips + 9 * (2 * width) + 8
+    limit = (24 << 20) + (total + 2 * W) * 4 * rows_i * 2 + rows_o * total * 2 + rows_o * channels * 72
     shape = jax.ShapeDtypeStruct
     grad, db, outputs, back = pl.pallas_call(
         functools.partial(kernel, (clips, bands, chans, rows_o, rows_i, cells, channels, scale)),
         out_shape=(
             shape((9, rows_o, channels), F32),
-            shape((8, rows_o), F32),
+            shape((1, rows_o), F32),
             shape((channels, cells), BF16),
-            shape((cells, channels), BF16),
+            shape((channels, cells), BF16),
         ),
-        in_specs=[VM] * 5,
+        in_specs=[VM] * 4,
         out_specs=(VM,) * 4,
         scratch_shapes=[
             pltpu.VMEM((total, rows_i), BF16),
@@ -376,13 +428,24 @@
             pltpu.VMEM((clips, 8, rows_o), F32),
             pltpu.VMEM((2, W, channels), BF16),
             pltpu.VMEM((2, W, channels), BF16),
+            pltpu.VMEM((cells, channels), BF16),
+            pltpu.VMEM((cells, channels), BF16),
             pltpu.SemaphoreType.DMA((2, copies)),
             pltpu.SemaphoreType.DMA((3,)),
         ],
-        compiler_params=pltpu.CompilerParams(collective_id=0, has_side_effects=True, vmem_limit_bytes=67000000),
-    )(x.T, g.T, g, wt, bias[:, None])
+        compiler_params=pltpu.CompilerParams(collective_id=0, has_side_effects=True, vmem_limit_bytes=min(67000000, limit)),
+    )(x, g, wt, bias[None, :])
+    results = (grad, db, outputs, back)
+    grad, db, outputs, back = pl.pallas_call(
+        emit,
+        out_shape=tuple(shape(r.shape, r.dtype) for r in results),
+        in_specs=[VM] * 4,
+        out_specs=(pl.BlockSpec(memory_space=pl.ANY),) * 4,
+        scratch_shapes=[pltpu.SemaphoreType.DMA((4,))],
+        compiler_params=pltpu.CompilerParams(vmem_limit_bytes=16 << 20),
+    )(*results)
     outputs = outputs.reshape(frames.shape)
-    grad_frames = back.T.reshape(frames.shape)
+    grad_frames = back.reshape(frames.shape)
     grad_weight = jnp.transpose(grad.reshape(3, 3, rows_o, channels), (2, 0, 1, 3))
     return outputs, grad_frames, grad_weight, db[0]
 

time: 124 us -> 105 us (0.85)
  local copies, waits for them, and re-layouts: 16.3 us -> 4.51 us
  Pallas kernels: 107 us -> 99.3 us
    pallas_call x1, Pallas kernels: 107 us -> 96.7 us  [local(): pl.pallas_call(functools.partial(kernel, (clips, bands, chans, rows_o, ro...]
    unnamed x4 -> x8, local copies, waits for them, and re-layouts: 11.3 us -> 4.51 us
    pallas_call x0 -> x1, Pallas kernels: none -> 2.63 us  [local(): pl.pallas_call(emit, out_shape=tuple((shape(r.shape, r.dtype) for r in re...]
    transpose x1 -> x0, local copies, waits for them, and re-layouts: 2.17 us -> none  [local(): grad, db, outputs, back = pl.pallas_call(functools.partial(kernel, (clips...]
    broadcast_in_dim x1 -> x0, local copies, waits for them, and re-layouts: 1.54 us -> none  [local(): bias[:, None]]
    slice x1 -> x0, local copies, waits for them, and re-layouts: 1.26 us -> none  [local(): return (outputs, grad_frames, grad_weight, db[0])]
where the time goes in v3:
time: 105 us; the launch traced here: 104 us
  Pallas kernels  99.3 us (95%)
  local copies, waits for them, and re-layouts  4.51 us (4%)
    pallas_call x1, Pallas kernels, local(): pl.pallas_call(functools.partial(kernel, (clips, bands, chans, rows_o, ro...  96.7 us
    unnamed x8, local copies, waits for them, and re-layouts  4.51 us
    pallas_call x1, Pallas kernels, local(): pl.pallas_call(emit, out_shape=tuple((shape(r.shape, r.dtype) for r in re...  2.63 us

profile of v3, /device:TPU:0, one launch (start us, length us, event | category | flops | bytes accessed | tf_op | source)
XLA Modules:
  0.0 104.5 jit_solution(12579061954756851904)
XLA Ops:
  0.6 0.0 copy-start
  0.6 1.7 %copy-done = bf16[256,3,3,512]{3,0,2,1:T(8,128)(2,1)S(1)} copy-done((bf16[256,3,3,512]{3,0,2,1:T(8,128)(2,1)S(1)}, bf16[256,3,3,512]{3,0,2,1:T(8,128)(2,1)}, u32[]{:S(2)}) %copy-start) | copy-done | bytes 2359320
  2.3 0.0 copy-start.1
  2.3 1.1 %copy-done.1 = bf16[512,1,640]{2,0,1:T(8,128)(2,1)S(1)} copy-done((bf16[512,1,640]{2,0,1:T(8,128)(2,1)S(1)}, bf16[512,1,640]{2,0,1:T(8,128)(2,1)}, u32[]{:S(2)}) %copy-start.1) | copy-done | bytes 655384
  3.4 0.0 copy-start.2
  3.4 1.1 %copy-done.2 = bf16[512,1,640]{2,0,1:T(8,128)(2,1)S(1)} copy-done((bf16[512,1,640]{2,0,1:T(8,128)(2,1)S(1)}, bf16[512,1,640]{2,0,1:T(8,128)(2,1)}, u32[]{:S(2)}) %copy-start.2) | copy-done | bytes 655384
  4.5 0.0 copy-start.3
  4.5 0.7 copy-done.3
  5.2 96.7 %shard_map.75 = (f32[9,256,512]{2,1,0:T(8,128)S(1)}, f32[1,256]{1,0:T(1,128)S(1)}, bf16[512,640]{1,0:T(8,128)(2,1)S(1)}, bf16[512,640]{1,0:T(8,128)(2,1)S(1)}) custom-call(bf16[512,640]{1,0:T(8,128)(2,1)S(1)} %bitcast.13, bf16[512,640]{1,0:T(8,128)(2,1)S(1)} %bitcast.14, bf16[9,256,512]{2,1,0:T(8,128)(2,1)S(1)} %bitcast.12, f32[1,512]{1,0:T(1,128)S(1)} %bitcast.15), custom_call_target="tpu_custom_call" | custom-call | tf_op jit(solution)/shard_map/pallas_call | solution.py:406
  101.8 2.6 %shard_map.76 = (f32[9,256,512]{2,1,0:T(8,128)}, f32[1,256]{1,0:T(1,128)}, bf16[512,640]{1,0:T(8,128)(2,1)}, bf16[512,640]{1,0:T(8,128)(2,1)}) custom-call(f32[9,256,512]{2,1,0:T(8,128)S(1)} %get-tuple-element.12.refs_0_, f32[1,256]{1,0:T(1,128)S(1)} %get-tuple-element.13.refs_1_, bf16[512,640]{1,0:T(8,128)(2,1)S(1)} %get-tuple-element.14.refs_2_, ...), custom_call_target="tpu_custom_call" | custom-call | tf_op jit(solution)/shard_map/pallas_call | solution.py:439
Async XLA Ops:
  0.6 1.7 %copy-start = (bf16[256,3,3,512]{3,0,2,1:T(8,128)(2,1)S(1)}, bf16[256,3,3,512]{3,0,2,1:T(8,128)(2,1)}, u32[]{:S(2)}) copy-start(bf16[256,3,3,512]{3,0,2,1:T(8,128)(2,1)} %param.5) | copy-start | bytes 7077892
  2.3 1.1 %copy-start.1 = (bf16[512,1,640]{2,0,1:T(8,128)(2,1)S(1)}, bf16[512,1,640]{2,0,1:T(8,128)(2,1)}, u32[]{:S(2)}) copy-start(bf16[512,1,640]{2,0,1:T(8,128)(2,1)} %param.4) | copy-start | bytes 1966084
  3.4 1.1 %copy-start.2 = (bf16[512,1,640]{2,0,1:T(8,128)(2,1)S(1)}, bf16[512,1,640]{2,0,1:T(8,128)(2,1)}, u32[]{:S(2)}) copy-start(bf16[512,1,640]{2,0,1:T(8,128)(2,1)} %param.7) | copy-start | bytes 1966084
  4.5 0.7 copy-start.3

commit v4 on v3

--- a/solution.py
+++ b/solution.py
@@ -33,8 +33,8 @@
 
 
 def kernel(
-    dims, x_ref, g_ref, w_ref, bias_ref, o_ref, db_ref, out_ref, back_ref,
-    xs, gs, dx, xe, ge, kern, acc, share, got1, got2, dbs, dgot, hx, hg, xt_ref, gt_ref, sems, regs,
+    dims, x_in, g_in, w_ref, bias_in, o_ref, db_ref, out_ref, back_ref,
+    xs, gs, dx, xe, ge, kern, acc, share, got1, got2, dbs, dgot, hx, hg, xt_ref, gt_ref, x_ref, g_ref, bias_ref, sems, regs,
 ):
     clips, bands, chans, rows_o, rows_i, cells, channels, scale = dims
     group = bands * chans
@@ -51,9 +51,16 @@
     nxt, prv = (me + 1) % group, (me + group - 1) % group
     nxt_id = {"band": nxt // chans, "chan": nxt % chans}
     prv_id = {"band": prv // chans, "chan": prv % chans}
-    z0, z1 = z % 2, z // 2
-    near, far = {"clip": z + 1 - 2 * z0}, {"clip": (z + 2) % clips}
-
+    z0 = z % 2
+    inner = (z + 1) // 2 == 1
+    near, middle = {"clip": z + 1 - 2 * z0}, {"clip": clips - 1 - z}
+
+    loads = [
+        pltpu.make_async_copy(src, dst, regs.at[3 + i])
+        for i, (src, dst) in enumerate(((x_in, x_ref), (g_in, g_ref), (bias_in, bias_ref)))
+    ]
+    for load in loads:
+        load.start()
     barrier = pltpu.get_barrier_semaphore()
     targets = [{"clip": (z + k) % clips} for k in range(1, clips)]
     for k in range(1, group):
@@ -67,7 +74,10 @@
         def _(t):
             dst[ds(t * 128, 128), :] = src[:, ds(t * 128, 128)].astype(F32).T.astype(BF16)
 
+    loads[0].wait()
     turn(x_ref, xt_ref)
+    loads[1].wait()
+    loads[2].wait()
     pl.semaphore_wait(barrier, len(targets))
 
     started = []
@@ -101,6 +111,8 @@
     def g_place(src_b, src_n):
         return gs.at[:, ds((src_b * chans + src_n) * cells, cells)]
 
+    for m in range(1, chans):
+        send(w_ref.at[:, ds(core * half, half), ds(z * lanes, lanes)], slab(n, core, z), ("w", m), {"chan": (n + m) % chans})
     for d in range(1, bands):
         to_b = (b + d) % bands
         send(xt_ref.at[:, ds(to_b * rows_i, rows_i)], x_place(b, n), ("x", d, 0), {"band": to_b})
@@ -108,8 +120,6 @@
         to_n = (n + m) % chans
         send(g_ref.at[ds(to_n * rows_o, rows_o), :], g_place(b, n), ("g", 0, m), {"chan": to_n})
         send(xt_ref.at[:, ds(b * rows_i, rows_i)], x_place(b, n), ("x", 0, m), {"chan": to_n})
-    for m in range(1, chans):
-        send(w_ref.at[:, ds(core * half, half), ds(z * lanes, lanes)], slab(n, core, z), ("w", m), {"chan": (n + m) % chans})
     own_g = g_ref.at[ds(n * rows_o, rows_o), :]
     for j in range(1, width):
         send(own_g, g_place(b, n), ("g", j, 0), {"band": (b + 2 * j) % bands})
@@ -128,6 +138,12 @@
             at = src * cells + u * W
             widen(dx, at + W, xs[ds(at, W), :], rows_i)
 
+    for m in range(1, chans):
+        src = (n + chans - m) % chans
+        arrive(slab(src, core, z), ("w", m))
+        for q in range(1, clips):
+            send(slab(src, core, z), slab(src, core, z), ("wz", m, q), {"clip": (z + q) % clips})
+        send(slab(src, core, z), slab(src, core, z), ("ws", m, 0), sib_id)
     for d in range(1, bands):
         place = x_place((b + bands - d) % bands, n)
         arrive(place, ("x", d, 0))
@@ -139,12 +155,6 @@
         for j in range(1, width):
             send(place, place, ("g", j, m), {"band": (b + 2 * j) % bands})
         send(place, place, ("f", 0, m), sib_id)
-    for m in range(1, chans):
-        src = (n + chans - m) % chans
-        arrive(slab(src, core, z), ("w", m))
-        for q in range(1, clips):
-            send(slab(src, core, z), slab(src, core, z), ("wz", m, q), {"clip": (z + q) % clips})
-        send(slab(src, core, z), slab(src, core, z), ("ws", m, 0), sib_id)
     for j in range(1, width):
         place = g_place((b + bands - 2 * j) % bands, n)
         arrive(place, ("g", j, 0))
@@ -199,64 +209,56 @@
 
         for t in range(3):
             share[3 * a + t] = acc2[:, t * rows_i:(t + 1) * rows_i] * scale
-        taps = pl.ds(3 * a, 3)
-        send(share.at[taps, ds((1 - z0) * half, half), :], got1.at[taps], ("r1", a), near)
-
-    quarter = half // 2
-
-    def spot(a, start, size, bb):
-        return o_ref.at[pl.ds(3 * a, 3), ds(start, size), ds(bb * rows_i, rows_i)]
-
-    def reduce1(a):
-        arrive(got1.at[pl.ds(3 * a, 3)], ("r1", a))
-        for t in range(3 * a, 3 * a + 3):
-            share[t, ds(z0 * half, half), :] += got1[t]
-        send(
-            share.at[pl.ds(3 * a, 3), ds((2 * z0 + 1 - z1) * quarter, quarter), :],
-            got2.at[pl.ds(3 * a, 3)], ("r2", a), far,
-        )
-
-    def spread(a, start, size, step):
-        place = spot(a, start, size, b)
+
+    side = z // 2
+
+    def spot(t, part, bb):
+        return o_ref.at[t, ds(part * half, half), ds(bb * rows_i, rows_i)]
+
+    def spread(t, part, step):
+        place = spot(t, part, b)
         for j in range(1, width):
-            send(place, place, ("xo", a, step, j), {"band": (b + 2 * j) % bands})
-        send(place, place, ("c", a, step, 0), sib_id)
-
-    mine = (2 * z0 + z1) * quarter
-    other = (2 * z0 + 1 - z1) * quarter
-
-    def reduce2(a):
-        arrive(got2.at[pl.ds(3 * a, 3)], ("r2", a))
-        for t in range(3 * a, 3 * a + 3):
-            o_ref[t, ds(mine, quarter), ds(b * rows_i, rows_i)] = share[t, ds(mine, quarter), :] + got2[t]
-        send(spot(a, mine, quarter, b), spot(a, mine, quarter, b), ("a1", a), far)
-        spread(a, mine, quarter, 0)
-
-    def gather1(a):
-        arrive(spot(a, other, quarter, b), ("a1", a))
-        send(spot(a, z0 * half, half, b), spot(a, z0 * half, half, b), ("a2", a), near)
-        spread(a, other, quarter, 1)
-
-    def gather2(a):
-        arrive(spot(a, (1 - z0) * half, half, b), ("a2", a))
-        spread(a, (1 - z0) * half, half, 2)
-
-    def regions(step):
-        return ((mine, quarter), (other, quarter), ((1 - z0) * half, half))[step]
-
-    def cross(a):
-        for step in range(3):
-            start, size = regions(step)
+            send(place, place, ("xo", t, step, j), {"band": (b + 2 * j) % bands})
+        send(place, place, ("c", t, step, 0), sib_id)
+
+    def give(t):
+        send(share.at[t], got1.at[t], ("r1", t), near)
+
+    def take(t):
+        arrive(got1.at[t], ("r1", t))
+        share[t] += got1[t]
+        send(share.at[t, ds((1 - side) * half, half), :], got2.at[t], ("r2", t), middle)
+
+    def settle(t):
+        arrive(got2.at[t], ("r2", t))
+        o_ref[t, ds(side * half, half), ds(b * rows_i, rows_i)] = share[t, ds(side * half, half), :] + got2[t]
+        place = spot(t, side, b)
+        send(place, place, ("a1", t), middle)
+        send(place, place, ("a2", t, 0), near)
+        spread(t, side, 0)
+
+    def share_back(t):
+        place = spot(t, 1 - side, b)
+        arrive(place, ("a1", t))
+        send(place, place, ("a2", t, 1), near)
+        spread(t, 1 - side, 1)
+
+    def receive(t):
+        for step, part in enumerate((side, 1 - side)):
+            arrive(spot(t, part, b), ("a2", t, step))
+            spread(t, part, step)
+
+    def cross(t):
+        for step, part in enumerate((side, 1 - side)):
             for j in range(1, width):
-                place = spot(a, start, size, (b + bands - 2 * j) % bands)
-                arrive(place, ("xo", a, step, j))
-                send(place, place, ("c", a, step, j), sib_id)
-
-    def finish(a):
-        for step in range(3):
-            start, size = regions(step)
+                place = spot(t, part, (b + bands - 2 * j) % bands)
+                arrive(place, ("xo", t, step, j))
+                send(place, place, ("c", t, step, j), sib_id)
+
+    def finish(t):
+        for step, part in enumerate((side, 1 - side)):
             for j in range(width):
-                arrive(spot(a, start, size, (sib + bands - 2 * j) % bands), ("c", a, step, j))
+                arrive(spot(t, part, (sib + bands - 2 * j) % bands), ("c", t, step, j))
 
     def conv(a):
         @pl.loop(0, channels // 256)
@@ -336,42 +338,59 @@
                 arrive(slab(src, 1 - core, (z + clips - q) % clips), ("ws", m, q))
         keep_w.wait()
 
-    tap_row(0)
-    tap_row(1)
-    reduce1(0)
-    tap_row(2)
-    bias_sum()
-    reduce1(1)
-    halos()
-    reduce2(0)
-    reduce1(2)
-    weights()
-    conv(0)
-    reduce2(1)
-    gather1(0)
-    conv(1)
-    reduce2(2)
-    gather1(1)
-    conv(2)
-    gather2(0)
-    gather1(2)
-    back(0)
-    gather2(1)
-    cross(0)
-    back(1)
-    gather2(2)
-    cross(1)
-    back(2)
-    cross(2)
-    for q in range(1, clips):
-        arrive(dgot.at[q], ("d", q))
-    sums = dbs[...]
-    for q in range(1, clips):
-        sums = sums + dgot[q]
-    db_ref[...] = sums[:1] * scale
-    for a in range(3):
-        finish(a)
-    for copy in started:
+    def matmuls():
+        yield halos()
+        yield weights()
+        for a in range(3):
+            yield conv(a)
+        for a in range(3):
+            yield back(a)
+
+    gathered = list(started)
+
+    def second_half(role):
+        started.clear()
+        work = matmuls()
+        for a in range(3):
+            tap_row(a)
+            if not role:
+                for t in range(3 * a, 3 * a + 3):
+                    give(t)
+        bias_sum()
+        if role:
+            for t in range(13):
+                for step, lag in ((take, 0), (settle, 1), (share_back, 2), (cross, 4)):
+                    if 0 <= t - lag < 9:
+                        step(t - lag)
+                next(work, None)
+        else:
+            for _ in range(4):
+                next(work)
+            for t in range(11):
+                for step, lag in ((receive, 0), (cross, 2)):
+                    if 0 <= t - lag < 9:
+                        step(t - lag)
+                next(work, None)
+        for q in range(1, clips):
+            arrive(dgot.at[q], ("d", q))
+        sums = dbs[...]
+        for q in range(1, clips):
+            sums = sums + dgot[q]
+        db_ref[...] = sums[:1] * scale
+        for t in range(9):
+            finish(t)
+        for copy in started:
+            copy.wait_send()
+
+    @pl.when(inner)
+    def _():
+        second_half(True)
+
+    @pl.when(jnp.logical_not(inner))
+    def _():
+        second_half(False)
+
+    for copy in gathered:
         copy.wait_send()
 
 
@@ -400,7 +419,7 @@
     wt = jnp.transpose(weight, (1, 2, 0, 3)).reshape(9, rows_o, channels)
     half = rows_o // 2
     width = bands // 2
-    copies = (chans - 1) * (1 + clips - 1 + clips) + 2 * width * chans + group + bands * chans + 4 + 12 + clips + 9 * (2 * width) + 8
+    copies = (chans - 1) * (1 + clips - 1 + clips) + 2 * width * chans + group + bands * chans + 4 + clips + 9 * (5 + 4 * width) + 8
     limit = (24 << 20) + (total + 2 * W) * 4 * rows_i * 2 + rows_o * total * 2 + rows_o * channels * 72
     shape = jax.ShapeDtypeStruct
     grad, db, outputs, back = pl.pallas_call(
@@ -411,7 +430,7 @@
             shape((channels, cells), BF16),
             shape((channels, cells), BF16),
         ),
-        in_specs=[VM] * 4,
+        in_specs=[pl.BlockSpec(memory_space=pltpu.HBM)] * 4,
         out_specs=(VM,) * 4,
         scratch_shapes=[
             pltpu.VMEM((total, rows_i), BF16),
@@ -422,16 +441,19 @@
             pltpu.VMEM((9, channels, channels), BF16),
             pltpu.VMEM((max(channels, cells), max(channels, cells)), F32),
             pltpu.VMEM((9, rows_o, rows_i), F32),
+            pltpu.VMEM((9, rows_o, rows_i), F32),
             pltpu.VMEM((9, half, rows_i), F32),
-            pltpu.VMEM((9, half // 2, rows_i), F32),
             pltpu.VMEM((8, rows_o), F32),
             pltpu.VMEM((clips, 8, rows_o), F32),
             pltpu.VMEM((2, W, channels), BF16),
             pltpu.VMEM((2, W, channels), BF16),
             pltpu.VMEM((cells, channels), BF16),
             pltpu.VMEM((cells, channels), BF16),
+            pltpu.VMEM((channels, cells), BF16),
+            pltpu.VMEM((channels, cells), BF16),
+            pltpu.VMEM((1, channels), F32),
             pltpu.SemaphoreType.DMA((2, copies)),
-            pltpu.SemaphoreType.DMA((3,)),
+            pltpu.SemaphoreType.DMA((6,)),
         ],
         compiler_params=pltpu.CompilerParams(collective_id=0, has_side_effects=True, vmem_limit_bytes=min(67000000, limit)),
     )(x, g, wt, bias[None, :])

time: 105 us -> 97 us (0.924)
  Pallas kernels: 99.3 us -> 91.6 us
    pallas_call x1, Pallas kernels: 96.7 us -> 89 us  [local(): pl.pallas_call(functools.partial(kernel, (clips, bands, chans, rows_o, ro...]
where the time goes in v4:
time: 97 us; the launch traced here: 96.8 us
  Pallas kernels  91.6 us (94%)
  local copies, waits for them, and re-layouts  4.51 us (5%)
    pallas_call x1, Pallas kernels, local(): pl.pallas_call(functools.partial(kernel, (clips, bands, chans, rows_o, ro...  89 us
    unnamed x8, local copies, waits for them, and re-layouts  4.51 us
    pallas_call x1, Pallas kernels, local(): pl.pallas_call(emit, out_shape=tuple((shape(r.shape, r.dtype) for r in re...  2.63 us

profile of v4, /device:TPU:0, one launch (start us, length us, event | category | flops | bytes accessed | tf_op | source)
XLA Modules:
  0.0 96.8 jit_solution(7988225366844220405)
XLA Ops:
  0.6 0.0 copy-start
  0.6 1.7 %copy-done = bf16[256,3,3,512]{3,0,2,1:T(8,128)(2,1)S(1)} copy-done((bf16[256,3,3,512]{3,0,2,1:T(8,128)(2,1)S(1)}, bf16[256,3,3,512]{3,0,2,1:T(8,128)(2,1)}, u32[]{:S(2)}) %copy-start) | copy-done | bytes 2359320
  2.3 0.0 copy-start.1
  2.3 1.1 %copy-done.1 = bf16[512,1,640]{2,0,1:T(8,128)(2,1)S(1)} copy-done((bf16[512,1,640]{2,0,1:T(8,128)(2,1)S(1)}, bf16[512,1,640]{2,0,1:T(8,128)(2,1)}, u32[]{:S(2)}) %copy-start.1) | copy-done | bytes 655384
  3.4 0.0 copy-start.2
  3.4 1.1 %copy-done.2 = bf16[512,1,640]{2,0,1:T(8,128)(2,1)S(1)} copy-done((bf16[512,1,640]{2,0,1:T(8,128)(2,1)S(1)}, bf16[512,1,640]{2,0,1:T(8,128)(2,1)}, u32[]{:S(2)}) %copy-start.2) | copy-done | bytes 655384
  4.5 0.0 copy-start.3
  4.5 0.7 copy-done.3
  5.2 89.0 %shard_map.75 = (f32[9,256,512]{2,1,0:T(8,128)S(1)}, f32[1,256]{1,0:T(1,128)S(1)}, bf16[512,640]{1,0:T(8,128)(2,1)S(1)}, bf16[512,640]{1,0:T(8,128)(2,1)S(1)}) custom-call(bf16[512,640]{1,0:T(8,128)(2,1)S(1)} %bitcast.13, bf16[512,640]{1,0:T(8,128)(2,1)S(1)} %bitcast.14, bf16[9,256,512]{2,1,0:T(8,128)(2,1)S(1)} %bitcast.12, f32[1,512]{1,0:T(1,128)S(1)} %bitcast.15), custom_call_target="tpu_custom_call" | custom-call | tf_op jit(solution)/shard_map/pallas_call | solution.py:425
  94.2 2.6 %shard_map.76 = (f32[9,256,512]{2,1,0:T(8,128)}, f32[1,256]{1,0:T(1,128)}, bf16[512,640]{1,0:T(8,128)(2,1)}, bf16[512,640]{1,0:T(8,128)(2,1)}) custom-call(f32[9,256,512]{2,1,0:T(8,128)S(1)} %get-tuple-element.12.refs_0_, f32[1,256]{1,0:T(1,128)S(1)} %get-tuple-element.13.refs_1_, bf16[512,640]{1,0:T(8,128)(2,1)S(1)} %get-tuple-element.14.refs_2_, ...), custom_call_target="tpu_custom_call" | custom-call | tf_op jit(solution)/shard_map/pallas_call | solution.py:461
Async XLA Ops:
  0.6 1.7 %copy-start = (bf16[256,3,3,512]{3,0,2,1:T(8,128)(2,1)S(1)}, bf16[256,3,3,512]{3,0,2,1:T(8,128)(2,1)}, u32[]{:S(2)}) copy-start(bf16[256,3,3,512]{3,0,2,1:T(8,128)(2,1)} %param.5) | copy-start | bytes 7077892
  2.3 1.1 %copy-start.1 = (bf16[512,1,640]{2,0,1:T(8,128)(2,1)S(1)}, bf16[512,1,640]{2,0,1:T(8,128)(2,1)}, u32[]{:S(2)}) copy-start(bf16[512,1,640]{2,0,1:T(8,128)(2,1)} %param.4) | copy-start | bytes 1966084
  3.4 1.1 %copy-start.2 = (bf16[512,1,640]{2,0,1:T(8,128)(2,1)S(1)}, bf16[512,1,640]{2,0,1:T(8,128)(2,1)}, u32[]{:S(2)}) copy-start(bf16[512,1,640]{2,0,1:T(8,128)(2,1)} %param.7) | copy-start | bytes 1966084
  4.5 0.7 copy-start.3

commit v5 on v4

--- a/solution.py
+++ b/solution.py
@@ -362,15 +362,17 @@
                 for step, lag in ((take, 0), (settle, 1), (share_back, 2), (cross, 4)):
                     if 0 <= t - lag < 9:
                         step(t - lag)
-                next(work, None)
+                if t >= 3:
+                    next(work, None)
         else:
-            for _ in range(4):
-                next(work)
             for t in range(11):
                 for step, lag in ((receive, 0), (cross, 2)):
                     if 0 <= t - lag < 9:
                         step(t - lag)
-                next(work, None)
+                if t >= 2:
+                    next(work, None)
+        for _ in work:
+            pass
         for q in range(1, clips):
             arrive(dgot.at[q], ("d", q))
         sums = dbs[...]

time: 97 us -> 93.7 us (0.966)
  Pallas kernels: 91.6 us -> 88.2 us
    pallas_call x1, Pallas kernels: 89 us -> 85.6 us  [local(): pl.pallas_call(functools.partial(kernel, (clips, bands, chans, rows_o, ro...]
where the time goes in v5:
time: 93.7 us; the launch traced here: 93.4 us
  Pallas kernels  88.2 us (94%)
  local copies, waits for them, and re-layouts  4.51 us (5%)
    pallas_call x1, Pallas kernels, local(): pl.pallas_call(functools.partial(kernel, (clips, bands, chans, rows_o, ro...  85.6 us
    unnamed x8, local copies, waits for them, and re-layouts  4.51 us
    pallas_call x1, Pallas kernels, local(): pl.pallas_call(emit, out_shape=tuple((shape(r.shape, r.dtype) for r in re...  2.63 us

profile of v5, /device:TPU:0, one launch (start us, length us, event | category | flops | bytes accessed | tf_op | source)
XLA Modules:
  0.0 93.4 jit_solution(10125400868554486635)
XLA Ops:
  0.6 0.0 copy-start
  0.6 1.7 %copy-done = bf16[256,3,3,512]{3,0,2,1:T(8,128)(2,1)S(1)} copy-done((bf16[256,3,3,512]{3,0,2,1:T(8,128)(2,1)S(1)}, bf16[256,3,3,512]{3,0,2,1:T(8,128)(2,1)}, u32[]{:S(2)}) %copy-start) | copy-done | bytes 2359320
  2.3 0.0 copy-start.1
  2.3 1.1 %copy-done.1 = bf16[512,1,640]{2,0,1:T(8,128)(2,1)S(1)} copy-done((bf16[512,1,640]{2,0,1:T(8,128)(2,1)S(1)}, bf16[512,1,640]{2,0,1:T(8,128)(2,1)}, u32[]{:S(2)}) %copy-start.1) | copy-done | bytes 655384
  3.4 0.0 copy-start.2
  3.4 1.1 %copy-done.2 = bf16[512,1,640]{2,0,1:T(8,128)(2,1)S(1)} copy-done((bf16[512,1,640]{2,0,1:T(8,128)(2,1)S(1)}, bf16[512,1,640]{2,0,1:T(8,128)(2,1)}, u32[]{:S(2)}) %copy-start.2) | copy-done | bytes 655384
  4.5 0.0 copy-start.3
  4.5 0.7 copy-done.3
  5.2 85.6 %shard_map.75 = (f32[9,256,512]{2,1,0:T(8,128)S(1)}, f32[1,256]{1,0:T(1,128)S(1)}, bf16[512,640]{1,0:T(8,128)(2,1)S(1)}, bf16[512,640]{1,0:T(8,128)(2,1)S(1)}) custom-call(bf16[512,640]{1,0:T(8,128)(2,1)S(1)} %bitcast.13, bf16[512,640]{1,0:T(8,128)(2,1)S(1)} %bitcast.14, bf16[9,256,512]{2,1,0:T(8,128)(2,1)S(1)} %bitcast.12, f32[1,512]{1,0:T(1,128)S(1)} %bitcast.15), custom_call_target="tpu_custom_call" | custom-call | tf_op jit(solution)/shard_map/pallas_call | solution.py:427
  90.8 2.6 %shard_map.76 = (f32[9,256,512]{2,1,0:T(8,128)}, f32[1,256]{1,0:T(1,128)}, bf16[512,640]{1,0:T(8,128)(2,1)}, bf16[512,640]{1,0:T(8,128)(2,1)}) custom-call(f32[9,256,512]{2,1,0:T(8,128)S(1)} %get-tuple-element.12.refs_0_, f32[1,256]{1,0:T(1,128)S(1)} %get-tuple-element.13.refs_1_, bf16[512,640]{1,0:T(8,128)(2,1)S(1)} %get-tuple-element.14.refs_2_, ...), custom_call_target="tpu_custom_call" | custom-call | tf_op jit(solution)/shard_map/pallas_call | solution.py:463
Async XLA Ops:
  0.6 1.7 %copy-start = (bf16[256,3,3,512]{3,0,2,1:T(8,128)(2,1)S(1)}, bf16[256,3,3,512]{3,0,2,1:T(8,128)(2,1)}, u32[]{:S(2)}) copy-start(bf16[256,3,3,512]{3,0,2,1:T(8,128)(2,1)} %param.5) | copy-start | bytes 7077892
  2.3 1.1 %copy-start.1 = (bf16[512,1,640]{2,0,1:T(8,128)(2,1)S(1)}, bf16[512,1,640]{2,0,1:T(8,128)(2,1)}, u32[]{:S(2)}) copy-start(bf16[512,1,640]{2,0,1:T(8,128)(2,1)} %param.4) | copy-start | bytes 1966084
  3.4 1.1 %copy-start.2 = (bf16[512,1,640]{2,0,1:T(8,128)(2,1)S(1)}, bf16[512,1,640]{2,0,1:T(8,128)(2,1)}, u32[]{:S(2)}) copy-start(bf16[512,1,640]{2,0,1:T(8,128)(2,1)} %param.7) | copy-start | bytes 1966084
  4.5 0.7 copy-start.3
